TPU v7x, 512 devices: a whole 4x4x16 slice. The times are simulated.
512 devices in a mesh: takers: 64 (over z, x), nodes: 8 (over y, core).
Axes of the slice: x: 4, y: 4, z: 16, core: 2. Of those that a mesh axis runs over, the one named last changes fastest.
Arguments:
- slopes: bfloat16 [3, 65536], P(None, 'takers'), may hold values from 0.29882812 to 1.5
- intercepts: bfloat16 [65536], P('takers'), may hold values from -3 to 3
- guessing: bfloat16 [65536], P('takers'), may hold values from 0.049804688 to 0.29882812
- responses: int32 [256, 12, 128, 128], P('takers'), may hold values from 0 to 2, as said below
- tile_items: int32 [256, 12], P('takers'), may hold values from 0 to 511, as said below
- tile_count: int32 [256], P('takers'), may hold values from 4 to 12, as said below
Outputs:
- new_params: float32 [4, 65536], P(None, 'takers')
- marginal: float32 [32768], P('takers')
- posterior_mean: float32 [3, 32768], P(None, 'takers')
Inputs may be any that keep to these rules, and one draw needn't show every extreme that they name: `tile_items`: within a row block the used slots name distinct item blocks; some row block uses all 12 slots. `tile_count`: some row block uses all 12 slots; slots at or beyond the count are ignored. `responses`: 0 means not answered, 1 a wrong answer, 2 a right answer; most entries are 0.
All inputs are finite; a program needn't handle non-finite values.
Results may differ from a plain program's by a relative error of at most 0.0041.
Values may be sent and summed in bfloat16 or wider, within the bound.
No kernel may reach another device: no remote copies, remote signals or barrier semaphores. Data moves between devices by JAX's collectives and lax.ppermute only.
A program may use at most 64 MiB of HBM per device.

v0:
```python
import jax
import jax.numpy as jnp
from jax import lax
from jax.sharding import PartitionSpec as P

NODES_1D = 16


def node_grid(first_node, how_many, grid_side):
    node_index = first_node + jnp.arange(how_many, dtype=jnp.int32)
    lattice = jnp.stack(
        [
            node_index // (grid_side * grid_side),
            node_index // grid_side % grid_side,
            node_index % grid_side,
        ]
    ).astype(jnp.float32)
    return -3.0 + 6.0 * lattice / (grid_side - 1)


def log_prior(node_points, grid_side):
    whole = node_grid(0, grid_side**3, grid_side)
    log_total = jnp.log(jnp.sum(jnp.exp(-0.5 * jnp.sum(whole * whole, axis=0))))
    return -0.5 * jnp.sum(node_points * node_points, axis=0) - log_total


def tile_logits(slope_blk, icpt_blk, node_points):
    return (
        slope_blk[:, 0, :, None] * node_points[0]
        + slope_blk[:, 1, :, None] * node_points[1]
        + slope_blk[:, 2, :, None] * node_points[2]
        + icpt_blk[:, :, None]
    )


def apply_update(summed, own_slopes, own_icpt):
    current = jnp.concatenate(
        [own_slopes.astype(jnp.float32), own_icpt.astype(jnp.float32)[None]], axis=0
    )
    return current + summed[:4] / (summed[4:] + 1.0)


def indicators(answers):
    right_b = (answers == 2).astype(jnp.bfloat16)
    answered_b = (answers > 0).astype(jnp.bfloat16)
    wrong_b = (answers == 1).astype(jnp.bfloat16)
    return (right_b, wrong_b, answered_b)


def local(slopes, intercepts, guessing, responses, tile_items, tile_count):
    grid_side = NODES_1D
    tile_size = responses.shape[-1]
    slot_count = responses.shape[1]
    nodes_here = grid_side**3 // lax.axis_size("nodes")
    node_points = node_grid(lax.axis_index("nodes") * nodes_here, nodes_here, grid_side)
    prior_here = log_prior(node_points, grid_side)
    features = jnp.concatenate([node_points, jnp.ones((1, nodes_here), jnp.float32)], axis=0)
    all_slopes, all_icpt, all_guess = (
        lax.all_gather(slopes, "takers", axis=1, tiled=True),
        lax.all_gather(intercepts, "takers", axis=0, tiled=True),
        lax.all_gather(guessing, "takers", axis=0, tiled=True),
    )
    blocks = all_icpt.shape[0] // tile_size
    slope_tab = all_slopes.astype(jnp.float32).reshape(3, blocks, tile_size)
    icpt_tab = all_icpt.astype(jnp.float32).reshape(blocks, tile_size)
    guess_tab = all_guess.astype(jnp.float32).reshape(blocks, tile_size)

    def tables(block_ids, filled):
        live_mask = (jnp.arange(slot_count, dtype=jnp.int32) < filled).astype(jnp.float32)[
            :, None, None
        ]
        slope_blk = jnp.transpose(slope_tab[:, block_ids], (1, 0, 2))
        logits = tile_logits(slope_blk, icpt_tab[block_ids], node_points)
        return (logits, guess_tab[block_ids][:, :, None], live_mask)

    def loglik_block(inputs):
        answers, block_ids, filled = inputs
        logits, guess_rate, live_mask = tables(block_ids, filled)
        correct = guess_rate + (1.0 - guess_rate) * jax.nn.sigmoid(logits)
        log_miss = jnp.log(1.0 - guess_rate) + jax.nn.log_sigmoid(-logits)
        log_right = (jnp.log(correct) * live_mask).astype(jnp.bfloat16)
        log_wrong = (log_miss * live_mask).astype(jnp.bfloat16)
        right_b, wrong_b, answered_b = indicators(answers)
        stacked_ind = jnp.stack([right_b, wrong_b])
        stacked_tab = jnp.stack([log_right, log_wrong])
        matched = lax.dot_general(
            stacked_ind,
            stacked_tab,
            (((0, 1, 3), (0, 1, 2)), ((), ())),
            preferred_element_type=jnp.float32,
        )
        return matched + prior_here

    loglik = lax.map(loglik_block, (responses, tile_items, tile_count)).reshape(-1, nodes_here)
    row_max = jnp.max(loglik, axis=1)
    global_max = lax.pmax(row_max, "nodes")
    weights = jnp.exp(loglik - global_max[:, None])
    moment_here = jnp.einsum("cq,tq->ct", node_points, weights, precision=lax.Precision.HIGHEST)
    row_mass, moment = lax.psum((jnp.sum(weights, axis=1), moment_here), "nodes")
    log_norm = global_max + jnp.log(row_mass)
    posterior_mean = moment / row_mass
    posterior = (
        jnp.exp(loglik - log_norm[:, None]).astype(jnp.bfloat16).reshape(-1, tile_size, nodes_here)
    )

    def stats_block(inputs):
        answers, block_ids, filled, post_blk = inputs
        logits, guess_rate, live_mask = tables(block_ids, filled)
        sig_pos = jax.nn.sigmoid(logits)
        sig_neg = jax.nn.sigmoid(-logits)
        correct = guess_rate + (1.0 - guess_rate) * sig_pos
        right_b, wrong_b, answered_b = indicators(answers)
        stacked_ind = jnp.stack([right_b, answered_b])
        both_mass = lax.dot_general(
            stacked_ind, post_blk, (((2,), (0,)), ((), ())), preferred_element_type=jnp.float32
        )
        correct_mass = both_mass[0]
        node_mass = both_mass[1]
        gradient = (correct_mass - node_mass * correct) * (sig_pos / correct) * live_mask
        fisher = node_mass * (1.0 - guess_rate) * sig_pos * sig_pos * sig_neg / correct * live_mask
        grad_terms = jnp.einsum("kiq,cq->kci", gradient, features, precision=lax.Precision.HIGHEST)
        fisher_terms = jnp.einsum(
            "kiq,cq->kci", fisher, features * features, precision=lax.Precision.HIGHEST
        )
        return jnp.concatenate([grad_terms, fisher_terms], axis=1)

    tile_stats = lax.map(stats_block, (responses, tile_items, tile_count, posterior))
    flat_stats = jnp.transpose(tile_stats, (2, 0, 1, 3)).reshape(8, -1, tile_size)
    item_totals = (
        jnp.zeros((8, blocks, tile_size), jnp.float32).at[:, tile_items.reshape(-1)].add(flat_stats)
    )
    item_totals = item_totals.reshape(8, blocks * tile_size)
    summed = lax.psum_scatter(item_totals, "takers", scatter_dimension=1, tiled=True)
    summed = lax.psum(summed, "nodes")
    new_params = apply_update(summed, slopes, intercepts)
    return (new_params, log_norm, posterior_mean)


def solution(mesh):
    in_specs = (
        P(None, "takers"),
        P("takers"),
        P("takers"),
        P("takers", None, None, None),
        P("takers", None),
        P("takers"),
    )
    out_specs = (P(None, "takers"), P("takers"), P(None, "takers"))
    return jax.shard_map(local, mesh=mesh, in_specs=in_specs, out_specs=out_specs, check_vma=False)
```

profile of v0, /device:TPU:1, one launch (start us, length us, event | category | flops | bytes accessed | tf_op | source)
XLA Modules:
  0.0 1166.1 jit_solution(3456560826222330985)
XLA Ops:
  10.2 80.8 %all_gather.9 = bf16[65536]{0:T(1024)(128)(2,1)S(1)} all-gather(bf16[1024]{0:T(1024)(128)(2,1)} %param.12), channel_id=1, replica_groups=mesh['takers'=64,'nodes'=8] {'takers'}, dimensions={0}, use_global_device_ids=true | all-gather | bytes 133120 | tf_op jit(solution)/shard_map/all_gather | solution.py:61
  91.0 72.1 %all_gather.11 = bf16[65536]{0:T(1024)(128)(2,1)S(1)} all-gather(bf16[1024]{0:T(1024)(128)(2,1)} %param.11), channel_id=1, replica_groups=mesh['takers'=64,'nodes'=8] {'takers'}, dimensions={0}, use_global_device_ids=true | all-gather | bytes 133120 | tf_op jit(solution)/shard_map/all_gather | solution.py:60
  163.1 72.0 %all_gather.10 = bf16[3,65536]{1,0:T(4,128)(2,1)S(1)} all-gather(bf16[3,1024]{1,0:T(4,128)(2,1)} %param.10), channel_id=1, replica_groups=mesh['takers'=64,'nodes'=8] {'takers'}, dimensions={1}, use_global_device_ids=true | all-gather | bytes 399360 | tf_op jit(solution)/shard_map/all_gather | solution.py:59
  235.3 36.9 %while.21 = (s32[]{:T(128)}, f32[4,128,512]{2,1,0:T(8,128)S(1)}, s32[4,12,128,128]{3,2,1,0:T(8,128)}, s32[4,12]{1,0:T(4,128)S(1)}, f32[512,128]{1,0:T(8,128)S(1)...) while((s32[]{:T(128)}, f32[4,128,512]{2,1,0:T(8,128)S(1)}, ...), condition=%wide.region_4.5_spmd, body=%wide.region_3.4_spmd.sunk | while | flops 423168576 | bytes 8348177 | solution.py:94
  239.8 4.2 multiply_convert_fusion.2
  249.0 4.2 multiply_convert_fusion.2
  258.2 4.2 multiply_convert_fusion.2
  267.5 4.2 multiply_convert_fusion.2
  272.4 90.1 %pmax.7 = f32[512]{0:T(512)S(1)} all-reduce(f32[512]{0:T(512)S(1)} %bitcast.192), channel_id=1, replica_groups=mesh['takers'=64,'nodes'=8] {'nodes'}, use_global_device_ids=true, to_apply=%region_6.7 | all-reduce | flops 512 | bytes 4096 | tf_op jit(solution)/shard_map/pmax | solution.py:96
  362.8 12.4 %psum.21 = f32[512]{0:T(512)S(1)} all-reduce(f32[512]{0:T(512)S(1)} %bitcast.193), channel_id=1, replica_groups=mesh['takers'=64,'nodes'=8] {'nodes'}, use_global_device_ids=true, to_apply=%region_8.9 | all-reduce | flops 512 | bytes 4096 | tf_op jit(solution)/shard_map/psum | solution.py:99
  376.3 69.3 %while.22 = (s32[]{:T(128)}, f32[4,12,8,128]{3,2,1,0:T(8,128)S(1)}, s32[4,12,128,128]{3,2,1,0:T(8,128)}, bf16[4,128,512]{2,1,0:T(8,128)(2,1)}, s32[4,12]{1,0:T(4...) while((s32[]{:T(128)}, f32[4,12,8,128]{3,2,1,0:T(8,128)S(1)}, ...), condition=%wide.region_10.11_spmd, body=%wide.region_9.10_spmd.sunk | while | flops 507263552 | bytes 27296860 | solution.py:127
  381.2 1.9 fusion.147
  383.0 5.1 fusion.152
  388.1 5.4 fusion.151
  400.4 5.1 fusion.152
  405.4 5.4 fusion.151
  417.7 5.1 fusion.152
  422.8 5.4 fusion.151
  433.1 1.9 fusion.147
  435.0 5.1 fusion.152
  440.1 5.4 fusion.151
  445.8 2.2 scatter_fusion
  450.6 674.2 %reduce-scatter.2.cloned.1.call-done = f32[8,1024]{1,0:T(8,128)} async-done(((f32[8,65536]{1,0:T(8,128)}), f32[8,1024]{1,0:T(8,128)}) %reduce-scatter.2.cloned.1.call-update) | async-done | bytes 32784 | tf_op jit(solution)/shard_map/reduce_scatter | solution.py:133
  1124.8 33.2 %all-reduce.1 = (f32[8,1024]{1,0:T(8,128)S(1)}, f32[3,512]{1,0:T(4,128)S(1)}) all-reduce(f32[8,1024]{1,0:T(8,128)} %reduce-scatter.2.cloned.1.call-done, f32[3,512]{1,0:T(4,128)S(1)} %fusion.109), channel_id=1, replica_groups=mesh['takers'=64,'nodes'=8] {'nodes'}, use_global_device_ids=true, to_apply=%region_13.14 | all-reduce | flops 9728 | bytes 77824 | tf_op jit(solution)/shard_map/psum | solution.py:134
  (192 shorter events, 50.6 us)
Async XLA Ops:
  7.2 228.1 %copy-start.12 = (s32[4,12]{1,0:T(4,128)S(1)}, s32[4,12]{1,0:T(4,128)}, u32[]{:S(2)}) copy-start(s32[4,12]{1,0:T(4,128)} %param.14) | copy-start | bytes 580
  7.2 228.1 %copy-start.14 = (s32[4]{0:T(128)S(1)}, s32[4]{0:T(128)}, u32[]{:S(2)}) copy-start(s32[4]{0:T(128)} %param.15) | copy-start | bytes 52
  7.2 1117.6 %reduce-scatter.2.cloned.1.call-start = ((), (), s32[]{:S(2)}) async-start(), calls=%async_computation.1 | async-start | bytes 2129920 | tf_op jit(solution)/shard_map/reduce_scatter | solution.py:133
  7.3 228.0 %copy-start.4 = (s32[1,512]{1,0:T(1,128)}, s32[1,512]{1,0:T(1,128)S(1)}, u32[]{:S(2)}) copy-start(s32[1,512]{1,0:T(1,128)S(1)} %and_select_fusion.7) | copy-start | bytes 6148
  7.3 1.4 copy-start.8
  7.3 228.0 %copy-start.6 = (s32[1,512]{1,0:T(1,128)}, s32[1,512]{1,0:T(1,128)S(1)}, u32[]{:S(2)}) copy-start(s32[1,512]{1,0:T(1,128)S(1)} %get-tuple-element.285) | copy-start | bytes 6148
  375.3 1.0 copy-start.11
  376.3 69.5 %copy-start.13 = (s32[48]{0:T(128)S(1)}, s32[48]{0:T(128)}, u32[]{:S(2)}) copy-start(s32[48]{0:T(128)} %fusion.108) | copy-start | bytes 580
  376.3 3.2 copy-start.1
  388.1 5.5 copy-start.2
  393.6 3.2 copy-start.1
  405.4 5.5 copy-start.2
  410.9 3.2 copy-start.1
  422.8 5.5 copy-start.2
  428.3 3.2 copy-start.1
  440.1 5.5 copy-start.2
  445.6 3.8 copy-start.10
  445.6 4.0 copy-start.5
  445.6 4.0 copy-start.7
  445.6 4.0 copy-start.9
  445.8 712.9 %copy-start.3 = (bf16[3,1024]{1,0:T(4,128)(2,1)S(1)}, bf16[3,1024]{1,0:T(4,128)(2,1)}, u32[]{:S(2)}) copy-start(bf16[3,1024]{1,0:T(4,128)(2,1)} %param.10) | copy-start | bytes 18436
  448.0 1.3 copy-start
Sparse Core Ops, SparseCore 0:
  449.5 675.2 reduce-scatter.1
where the time goes:
time: 1170 us
  waiting for transfers between devices  674 us (58%)
  blocking collectives  361 us (31%)
  matrix products  52.9 us (5%)
  other arithmetic  35.2 us (3%)
  local copies, waits for them, and re-layouts  27.2 us (2%)
  between operations  15 us (1%)
    reduce_scatter x1, waiting for transfers between devices, local(): lax.psum_scatter(item_totals, 'takers', scatter_dimension=1, tiled=True)  674 us
    pmax x1, blocking collectives, local(): global_max = lax.pmax(row_max, 'nodes')  90.1 us
    all_gather x1, blocking collectives, local(): lax.all_gather(guessing, 'takers', axis=0, tiled=True)  80.8 us
    all_gather x1, blocking collectives, local(): lax.all_gather(intercepts, 'takers', axis=0, tiled=True)  72.1 us
    all_gather x1, blocking collectives, local(): lax.all_gather(slopes, 'takers', axis=1, tiled=True)  72 us
    psum x1, blocking collectives, local(): summed = lax.psum(summed, 'nodes')  33.2 us
  transfers between devices with their start and end apart: 1, of which 1 were waited for; matrix products, arithmetic and copies ran while one was open for 0% of the time, Pallas kernels for 0%

commit v1 on v0

v1 whole, which is shorter than its diff:
```python
import functools
import math

import jax
import jax.numpy as jnp
import numpy as np
from jax import lax
from jax.experimental import pallas as pl
from jax.experimental.pallas import tpu as pltpu
from jax.sharding import PartitionSpec as P

SIDE = 16
HALF = SIDE // 2
TILE = 128
KT = 12
SLOTS = 16
F32 = jnp.float32
BF16 = jnp.bfloat16

AXIS = (np.float32(-3.0) + np.float32(6.0) * np.arange(SIDE, dtype=np.float32) / np.float32(15.0)).astype(np.float32)
STEP = 6.0 / 15.0
LOG_TOTAL = 3.0 * math.log(float(np.sum(np.exp(-0.5 * AXIS.astype(np.float64) ** 2))))


def axis_column():
    index = lax.broadcasted_iota(jnp.int32, (SIDE, TILE), 0).astype(F32)
    return -3.0 + 6.0 * index / 15.0


def tile_start(par_ref, k, first):
    a0, a1, a2, d, c = (par_ref[j, pl.ds(k, 1), :] for j in range(5))
    base = jnp.exp(a2 * axis_column() + (a0 * first + a1 * float(AXIS[0]) + d))
    ratio0 = jnp.broadcast_to(jnp.exp(a0 * STEP), (SIDE, TILE))
    ratio1 = jnp.broadcast_to(jnp.exp(a1 * STEP), (SIDE, TILE))
    return base, ratio0, ratio1, c


def likelihood_kernel(sc_ref, got_ref, resp_ref, w_ref, st_ref, par_ref, tab_ref):
    count = sc_ref[1]
    first = -3.0 + STEP * HALF * sc_ref[2].astype(F32)
    par_ref[...] = got_ref[...].astype(F32)
    theta2 = axis_column()
    for j0 in range(HALF):
        theta0 = first + STEP * j0
        for j1 in range(SIDE):
            rows = pl.ds((j0 * SIDE + j1) * SIDE, SIDE)
            w_ref[rows, :] = -0.5 * (theta2 * theta2) - (
                0.5 * (theta0 * theta0) + (0.5 * float(AXIS[j1]) ** 2 + LOG_TOTAL)
            )

    def tile(k, carry):
        codes = jnp.transpose(resp_ref[0, k].astype(F32))
        marks = jnp.concatenate([(codes == 2.0).astype(BF16), (codes == 1.0).astype(BF16)], axis=0)
        base, ratio0, ratio1, c = tile_start(par_ref, k, first)
        c_b = jnp.broadcast_to(c, (SIDE, TILE))
        log_rest = jnp.broadcast_to(jnp.log(1.0 - c), (SIDE, TILE))
        for j0 in range(HALF):
            u = base
            for j1 in range(SIDE):
                rows = pl.ds((j0 * SIDE + j1) * SIDE, SIDE)
                log_one = jnp.log(1.0 + u)
                tab_ref[rows, 0:TILE] = (jnp.log(c_b + u) - log_one).astype(BF16)
                tab_ref[rows, TILE : 2 * TILE] = (log_rest - log_one).astype(BF16)
                u = u * ratio1
            slab = pl.ds(j0 * SIDE * SIDE, SIDE * SIDE)
            w_ref[slab, :] += jnp.dot(tab_ref[slab, :], marks, preferred_element_type=F32)
            base = base * ratio0
        return carry

    lax.fori_loop(0, count, tile, 0)

    top = jnp.full((SIDE, TILE), -jnp.inf, F32)
    for j in range(HALF * SIDE):
        top = jnp.maximum(top, w_ref[pl.ds(j * SIDE, SIDE), :])
    top = jnp.max(top, axis=0, keepdims=True)
    total = jnp.zeros((SIDE, TILE), F32)
    mom0 = jnp.zeros((SIDE, TILE), F32)
    mom1 = jnp.zeros((SIDE, TILE), F32)
    for j0 in range(HALF):
        slab_sum = jnp.zeros((SIDE, TILE), F32)
        for j1 in range(SIDE):
            rows = pl.ds((j0 * SIDE + j1) * SIDE, SIDE)
            w = jnp.exp(w_ref[rows, :] - top)
            w_ref[rows, :] = w
            slab_sum = slab_sum + w
            mom1 = mom1 + float(AXIS[j1]) * w
        total = total + slab_sum
        mom0 = mom0 + (first + STEP * j0) * slab_sum
    mom2 = total * theta2
    st_ref[0:1, :] = top
    for j, part in enumerate((total, mom0, mom1, mom2)):
        st_ref[j + 1 : j + 2, :] = jnp.sum(part, axis=0, keepdims=True)
    st_ref[5:8, :] = jnp.zeros((3, TILE), F32)


def statistics_kernel(sc_ref, got_ref, resp_ref, w_ref, mine_ref, other_ref, out_ref, par_ref, post_ref):
    count = sc_ref[1]
    first = -3.0 + STEP * HALF * sc_ref[2].astype(F32)
    par_ref[...] = got_ref[...].astype(F32)
    mine, other = mine_ref[...], other_ref[...]
    top = jnp.maximum(mine[0:1], other[0:1])
    both = mine[1:5] * jnp.exp(mine[0:1] - top) + other[1:5] * jnp.exp(other[0:1] - top)
    log_norm = top + jnp.log(both[0:1])
    means = both[1:4] / both[0:1]
    scale = jnp.exp(mine[0:1] - log_norm)
    post_ref[...] = (w_ref[...] * scale).astype(BF16)
    out_ref[...] = jnp.zeros(out_ref.shape, F32)
    for j in range(8):
        out_ref[j, KT : KT + 1, :] = log_norm
        out_ref[j, KT + 1 : KT + 4, :] = means
    theta2 = axis_column()

    def tile(k, carry):
        codes = resp_ref[0, k]
        marks = jnp.concatenate([(codes == 2).astype(BF16), (codes > 0).astype(BF16)], axis=1)
        base, ratio0, ratio1, c = tile_start(par_ref, k, first)
        c_b = jnp.broadcast_to(c, (SIDE, TILE))
        zero = jnp.zeros((SIDE, TILE), F32)
        g_all, f_all, g_0, f_0, g_1, f_1 = (zero,) * 6
        for j0 in range(HALF):
            slab = pl.ds(j0 * SIDE * SIDE, SIDE * SIDE)
            counts = jnp.dot(post_ref[slab, :], marks, preferred_element_type=F32)
            theta0 = first + STEP * j0
            u = base
            g_slab, f_slab = zero, zero
            for j1 in range(SIDE):
                hits = counts[j1 * SIDE : (j1 + 1) * SIDE, 0:TILE]
                mass = counts[j1 * SIDE : (j1 + 1) * SIDE, TILE : 2 * TILE]
                one_u = 1.0 + u
                c_u = c_b + u
                inv = 1.0 / (one_u * c_u)
                share = u * one_u * inv
                miss = c_u * inv
                mass_sig = mass * (u * miss)
                grad = hits * share - mass_sig
                info = mass_sig * (share * miss)
                g_slab, f_slab = g_slab + grad, f_slab + info
                g_1 = g_1 + float(AXIS[j1]) * grad
                f_1 = f_1 + float(AXIS[j1]) ** 2 * info
                u = u * ratio1
            g_all, f_all = g_all + g_slab, f_all + f_slab
            g_0, f_0 = g_0 + theta0 * g_slab, f_0 + (theta0 * theta0) * f_slab
            base = base * ratio0
        rest = 1.0 - c
        rows = (g_0, g_1, theta2 * g_all, g_all, f_0, f_1, (theta2 * theta2) * f_all, f_all)
        for j, part in enumerate(rows):
            summed = jnp.sum(part, axis=0, keepdims=True)
            out_ref[j, pl.ds(k, 1), :] = summed if j < 4 else summed * rest
        return carry

    lax.fori_loop(0, count, tile, 0)


def scatter_kernel(items_ref, count_ref, got_ref, out_ref, marg_ref, mean_ref, acc_ref):
    acc_ref[...] = jnp.zeros(acc_ref.shape, F32)
    for b in range(4):
        marg_ref[0:1, b * TILE : (b + 1) * TILE] = got_ref[2 * b, KT : KT + 1, :]
        mean_ref[:, b * TILE : (b + 1) * TILE] = got_ref[2 * b, KT + 1 : KT + 4, :]

        def slot(k, carry):
            row = pl.ds(items_ref[b, k], 1)
            acc_ref[row, :] += got_ref[2 * b, pl.ds(k, 1), :] + got_ref[2 * b + 1, pl.ds(k, 1), :]
            return carry

        lax.fori_loop(0, count_ref[b], slot, 0)
    out_ref[...] = acc_ref[...].astype(BF16)


def local(slopes, intercepts, guessing, responses, tile_items, tile_count):
    takers = lax.axis_size("takers")
    place = lax.axis_index("nodes")
    block, core = place // 2, place % 2
    own = slopes.shape[1]
    blocks = takers * own // TILE
    params = jnp.concatenate([slopes, intercepts[None], guessing[None], jnp.zeros((3, own), BF16)], axis=0)
    mine = lax.dynamic_index_in_dim(params, place, 0, keepdims=False)
    table = lax.all_to_all(jnp.broadcast_to(mine[None], (takers, own)), "takers", 0, 0).reshape(blocks, TILE)
    wanted = jnp.pad(tile_items, ((0, 0), (0, SLOTS - KT)))
    wanted = jnp.repeat(wanted, 2, axis=0).reshape(-1)
    pick = (wanted[:, None] == jnp.arange(blocks, dtype=jnp.int32)[None]).astype(BF16)
    picked = jnp.dot(pick, table, preferred_element_type=F32).astype(BF16).reshape(8, SLOTS, TILE)
    got = lax.all_to_all(picked, "nodes", 0, 0)

    scalars = jnp.stack([block, tile_count[block], core])
    nodes_here = HALF * SIDE * SIDE
    whole = pl.BlockSpec(memory_space=pltpu.VMEM)
    resp_spec = pl.BlockSpec((1, KT, TILE, TILE), lambda i, sc: (sc[0], 0, 0, 0))
    weights, state = pl.pallas_call(
        likelihood_kernel,
        out_shape=(jax.ShapeDtypeStruct((nodes_here, TILE), F32), jax.ShapeDtypeStruct((8, TILE), F32)),
        grid_spec=pltpu.PrefetchScalarGridSpec(
            num_scalar_prefetch=1,
            grid=(1,),
            in_specs=[whole, resp_spec],
            out_specs=(whole, whole),
            scratch_shapes=[
                pltpu.VMEM((8, SLOTS, TILE), F32),
                pltpu.VMEM((nodes_here, 2 * TILE), BF16),
            ],
        ),
        name="likelihood",
    )(scalars, got, responses)
    other = lax.ppermute(state, "nodes", [(i, i ^ 1) for i in range(8)])
    stats = pl.pallas_call(
        statistics_kernel,
        out_shape=jax.ShapeDtypeStruct((8, SLOTS, TILE), F32),
        grid_spec=pltpu.PrefetchScalarGridSpec(
            num_scalar_prefetch=1,
            grid=(1,),
            in_specs=[whole, resp_spec, whole, whole, whole],
            out_specs=whole,
            scratch_shapes=[
                pltpu.VMEM((8, SLOTS, TILE), F32),
                pltpu.VMEM((nodes_here, TILE), BF16),
            ],
        ),
        name="statistics",
    )(scalars, got, responses, weights, state, other)
    partial = lax.all_to_all(stats, "nodes", 0, 0)
    spread, marginal, means = pl.pallas_call(
        scatter_kernel,
        out_shape=(
            jax.ShapeDtypeStruct((blocks, TILE), BF16),
            jax.ShapeDtypeStruct((1, 4 * TILE), F32),
            jax.ShapeDtypeStruct((3, 4 * TILE), F32),
        ),
        grid_spec=pltpu.PrefetchScalarGridSpec(
            num_scalar_prefetch=2,
            grid=(1,),
            in_specs=[whole],
            out_specs=(whole, whole, whole),
            scratch_shapes=[pltpu.VMEM((blocks, TILE), F32)],
        ),
        name="spread",
    )(tile_items, tile_count, partial)
    owned = lax.all_to_all(spread.reshape(takers, own // TILE, TILE), "takers", 0, 0)
    summed = jnp.sum(owned.astype(F32), axis=0)
    all_stats = lax.all_to_all(jnp.broadcast_to(summed[None], (8,) + summed.shape), "nodes", 0, 0)
    all_stats = all_stats.reshape(8, own)
    current = jnp.concatenate([slopes.astype(F32), intercepts.astype(F32)[None]], axis=0)
    new_params = current + all_stats[:4] / (all_stats[4:] + 1.0)
    return new_params, marginal.reshape(-1), means


def solution(mesh):
    in_specs = (
        P(None, "takers"),
        P("takers"),
        P("takers"),
        P("takers", None, None, None),
        P("takers", None),
        P("takers"),
    )
    out_specs = (P(None, "takers"), P("takers"), P(None, "takers"))
    return jax.shard_map(local, mesh=mesh, in_specs=in_specs, out_specs=out_specs, check_vma=False)
```

time: 1170 us -> 127 us (0.11)
  waiting for transfers between devices: 674 us -> 17.3 us
  blocking collectives: 361 us -> 49.4 us
  matrix products: 52.9 us -> 0.84 us
  starting transfers between devices: 0.04 us -> 30.1 us
  other arithmetic: 35.2 us -> 5.5 us
  local copies, waits for them, and re-layouts: 27.2 us -> 6.72 us
  Pallas kernels: 0 us -> 16.1 us
  between operations: 15 us -> 0.72 us
    reduce_scatter x1 -> x0, waiting for transfers between devices: 674 us -> none  [local(): lax.psum_scatter(item_totals, 'takers', scatter_dimension=1, tiled=True)]
    all_gather x3 -> x0, blocking collectives: 225 us -> none  [the longest x1 80.8 us: local(): lax.all_gather(guessing, 'takers', axis=0, tiled=True)]
    pmax x1 -> x0, blocking collectives: 90.1 us -> none  [local(): global_max = lax.pmax(row_max, 'nodes')]
    dot_general x17 -> x1, matrix products: 52.9 us -> 0.84 us  [local(): jnp.dot(pick, table, preferred_element_type=F32).astype(BF16)]
    all_to_all x0 -> x3, blocking collectives: none -> 49.4 us  [the longest x1 21.8 us: local(): lax.all_to_all(spread.reshape(takers, own // TILE, TILE), 'takers', 0, 0)]
    psum x2 -> x0, blocking collectives: 45.7 us -> none  [the longest x1 33.2 us: local(): summed = lax.psum(summed, 'nodes')]
    all_to_all x0 -> x2, starting transfers between devices: none -> 27.3 us  [the longest x1 19.1 us: local(): lax.all_to_all(jnp.broadcast_to(mine[None], (takers, own)), 'takers', 0, 0)]
    convert_element_type x13 -> x0, other arithmetic: 22.8 us -> none  [the longest x4 16.7 us: loglik_block(): log_right = (jnp.log(correct) * live_mask).astype(jnp.bfloat16)]
  transfers between devices with their start and end apart: 1 -> 3, of which waited for: 1 -> 3; matrix products, arithmetic and copies ran while one was open for 0% -> 3% of each run, Pallas kernels for 0% -> 0%
where the time goes in v1:
time: 127 us
  blocking collectives  49.4 us (39%)
  starting transfers between devices  30.1 us (24%)
  waiting for transfers between devices  17.3 us (14%)
  Pallas kernels  16.1 us (13%)
  local copies, waits for them, and re-layouts  6.72 us (5%)
  other arithmetic  5.5 us (4%)
    all_to_all x1, blocking collectives, local(): lax.all_to_all(spread.reshape(takers, own // TILE, TILE), 'takers', 0, 0)  21.8 us
    all_to_all x1, starting transfers between devices, local(): lax.all_to_all(jnp.broadcast_to(mine[None], (takers, own)), 'takers', 0, 0)  19.1 us
    all_to_all x1, blocking collectives, local(): partial = lax.all_to_all(stats, 'nodes', 0, 0)  16.8 us
    all_to_all x1, waiting for transfers between devices, local(): lax.all_to_all(jnp.broadcast_to(mine[None], (takers, own)), 'takers', 0, 0)  12.9 us
    all_to_all x1, blocking collectives, local(): lax.all_to_all(jnp.broadcast_to(summed[None], (8,) + summed.shape), 'node...  10.7 us
    all_to_all x1, starting transfers between devices, local(): got = lax.all_to_all(picked, 'nodes', 0, 0)  8.2 us
    pallas_call x1, Pallas kernels, local(): pl.pallas_call(statistics_kernel, out_shape=jax.ShapeDtypeStruct((8, SLOT...  6.99 us
    pallas_call x1, Pallas kernels, local(): pl.pallas_call(likelihood_kernel, out_shape=(jax.ShapeDtypeStruct((nodes_...  6.67 us
  transfers between devices with their start and end apart: 3, of which 3 were waited for; matrix products, arithmetic and copies ran while one was open for 3% of the time, Pallas kernels for 0%

profile of v1, /device:TPU:1, one launch (start us, length us, event | category | flops | bytes accessed | tf_op | source)
XLA Modules:
  0.0 126.6 jit_solution(9561663962081957543)
XLA Ops:
  0.6 0.7 broadcast_in_dim.13
  1.3 0.7 broadcast_in_dim.29
  2.6 1.4 %maximum_reduce_fusion = bf16[1024]{0:T(1024)(128)(2,1)S(1)} fusion(s32[]{:T(128)S(6)} %select_n.21, bf16[1,1024]{1,0:T(2,128)(2,1)S(1)} %broadcast_in_dim.29, bf16[1,1024]{1,0:T(2,128)(2,1)S(1)} %broadcast_in_dim.13, bf16[3,1024]{1,0:T(4,128)(2,1)} %param.6, bf16[1]{0:T(256)(128)(2,1)} %pad_dynamic-slice_fusion.3), kind=kLoop, calls=%fused_computation.13 | loop fusion | flops 8192 | bytes 12294 | tf_op jit(solution)/shard_map/jit(dynamic_index_in_dim)/dynamic_slice | solution.py:176
  4.7 1.4 %reduce.3 = bf16[64,1024]{1,0:T(8,128)(2,1)S(1)} reduce(bf16[64,1,1024]{2,1,0:T(2,128)(2,1)S(1)} %broadcast_in_dim.31, bf16[]{:T(256)} %broadcast.16), dimensions={1}, to_apply=%broadcast_in_dim.31.reduce_sub_computation | reduce | bytes 262146 | tf_op jit(solution)/shard_map/broadcast_in_dim | solution.py:177
  6.0 0.7 reshape.39
  6.8 19.1 %all-to-all-start = ((bf16[64,2,512]{2,1,0:T(2,128)(2,1)}), bf16[64,2,512]{2,1,0:T(2,128)(2,1)S(1)}, u32[]{:S(2)}, u32[]{:S(2)}) async-start(bf16[64,2,512]{2,1,0:T(2,128)(2,1)} %reshape.39), calls=%async_computation | async-start | bytes 262144 | tf_op jit(solution)/shard_map/all_to_all | solution.py:177
  25.9 0.7 pad.4
  26.7 1.2 dynamic_slice.9
  27.9 12.9 %all-to-all-done = bf16[64,2,512]{2,1,0:T(2,128)(2,1)S(1)} async-done(((bf16[64,2,512]{2,1,0:T(2,128)(2,1)}), bf16[64,2,512]{2,1,0:T(2,128)(2,1)S(1)}, u32[]{:S(2)}, u32[]{:S(2)}) %all-to-all-start) | async-done | bytes 131104 | tf_op jit(solution)/shard_map/all_to_all | solution.py:177
  40.9 0.7 reduce.1
  41.7 0.8 convolution_convert_fusion
  42.5 8.2 %all-to-all-start.1 = ((bf16[8,16,128]{2,1,0:T(8,128)(2,1)}), bf16[8,16,128]{2,1,0:T(8,128)(2,1)S(1)}, u32[]{:S(2)}, u32[]{:S(2)}) async-start(bf16[8,16,128]{2,1,0:T(8,128)(2,1)} %bitcast.2), calls=%async_computation.1 | async-start | bytes 65536 | tf_op jit(solution)/shard_map/all_to_all | solution.py:182
  50.7 1.3 %pad_add_fusion.sc_ref = s32[3]{0:T(128)} fusion(s32[1]{0:T(128)} %bitcast.1, s32[1]{0:T(128)} %dynamic_slice.9, s32[1]{0:T(128)} %bitcast), kind=kLoop, calls=%fused_computation.15 | loop fusion | flops 6 | bytes 24 | tf_op jit(solution)/shard_map/stack | solution.py:184
  52.0 3.4 %all-to-all-done.1.got_ref = bf16[8,16,128]{2,1,0:T(8,128)(2,1)S(1)} async-done(((bf16[8,16,128]{2,1,0:T(8,128)(2,1)}), bf16[8,16,128]{2,1,0:T(8,128)(2,1)S(1)}, u32[]{:S(2)}, u32[]{:S(2)}) %all-to-all-start.1) | async-done | bytes 32800 | tf_op jit(solution)/shard_map/all_to_all | solution.py:182
  55.4 0.6 copy-done
  56.1 6.7 %likelihood.1 = (f32[2048,128]{1,0:T(8,128)}, f32[8,128]{1,0:T(8,128)}) custom-call(s32[3]{0:T(128)} %pad_add_fusion.sc_ref, bf16[8,16,128]{2,1,0:T(8,128)(2,1)} %copy-done, s32[4,12,128,128]{3,2,1,0:T(8,128)} %resp_ref.3), custom_call_target="tpu_custom_call" | custom-call | tf_op jit(solution)/shard_map/likelihood/pallas_call | solution.py:188
  62.7 2.8 %collective-permute-start = (f32[8,128]{1,0:T(8,128)}, f32[8,128]{1,0:T(8,128)S(1)}, u32[]{:S(2)}, u32[]{:S(2)}) collective-permute-start(f32[8,128]{1,0:T(8,128)} %get-tuple-element.9.mine_ref), channel_id=1, source_target_pairs={{0,1},{1,0},{2,3},{3,2},{4,5},{5,4},{6,7},{7,6},{8,9},{9,8},{10,11... | collective-permute-start | bytes 12296 | tf_op jit(solution)/shard_map/ppermute | solution.py:203
  65.5 1.0 collective-permute-done.other_ref
  67.1 7.0 %statistics.1 = f32[8,16,128]{2,1,0:T(8,128)} custom-call(s32[3]{0:T(128)} %pad_add_fusion.sc_ref, bf16[8,16,128]{2,1,0:T(8,128)(2,1)} %copy-done, s32[4,12,128,128]{3,2,1,0:T(8,128)} %resp_ref.3, f32[2048,128]{1,0:T(8,128)} %get-tuple-element.8.w_ref, f32[8,128]{1,0:T(8,128)} %get-tuple-element.9.mine_ref, f32[8,128]{1,0:T(8,128)} %copy-done.2), custom_call_target="tpu_custom_call" | custom-call | tf_op jit(solution)/shard_map/statistics/pallas_call | solution.py:204
  74.1 16.8 %all_to_all.26.got_ref = f32[8,16,128]{2,1,0:T(8,128)} all-to-all(f32[8,16,128]{2,1,0:T(8,128)} %statistics.1), channel_id=1, replica_groups=mesh['takers'=64,'nodes'=8] {'nodes'}, dimensions={0} | all-to-all | bytes 131072 | tf_op jit(solution)/shard_map/all_to_all | solution.py:219
  90.9 2.5 %spread.1 = (bf16[512,128]{1,0:T(8,128)(2,1)}, f32[1,512]{1,0:T(1,128)}, f32[3,512]{1,0:T(4,128)}) custom-call(s32[4,12]{1,0:T(4,128)} %items_ref.1, s32[4]{0:T(128)} %count_ref.1, f32[8,16,128]{2,1,0:T(8,128)} %all_to_all.26.got_ref), custom_call_target="tpu_custom_call" | custom-call | tf_op jit(solution)/shard_map/spread/pallas_call | solution.py:220
  93.4 21.8 %all_to_all.27 = bf16[64,8,128]{2,1,0:T(8,128)(2,1)S(1)} all-to-all(bf16[64,8,128]{2,1,0:T(8,128)(2,1)} %bitcast.10), channel_id=1, replica_groups=mesh['takers'=64,'nodes'=8] {'takers'}, dimensions={0} | all-to-all | bytes 262144 | tf_op jit(solution)/shard_map/all_to_all | solution.py:236
  115.3 10.7 %all_to_all.28 = f32[8,8,128]{2,1,0:T(8,128)S(1)} all-to-all(f32[8,8,128]{2,1,0:T(8,128)S(1)} %broadcast_in_dim.32), channel_id=1, replica_groups=mesh['takers'=64,'nodes'=8] {'nodes'}, dimensions={0} | all-to-all | bytes 65536 | tf_op jit(solution)/shard_map/all_to_all | solution.py:238
  126.0 0.6 bitcast_add_fusion
  (16 shorter events, 2.2 us)
Async XLA Ops:
  6.8 34.0 %all-to-all-start = ((bf16[64,2,512]{2,1,0:T(2,128)(2,1)}), bf16[64,2,512]{2,1,0:T(2,128)(2,1)S(1)}, u32[]{:S(2)}, u32[]{:S(2)}) async-start(bf16[64,2,512]{2,1,0:T(2,128)(2,1)} %reshape.39), calls=%async_computation | async-start | bytes 262144 | tf_op jit(solution)/shard_map/all_to_all | solution.py:177
  42.5 12.9 %all-to-all-start.1 = ((bf16[8,16,128]{2,1,0:T(8,128)(2,1)}), bf16[8,16,128]{2,1,0:T(8,128)(2,1)S(1)}, u32[]{:S(2)}, u32[]{:S(2)}) async-start(bf16[8,16,128]{2,1,0:T(8,128)(2,1)} %bitcast.2), calls=%async_computation.1 | async-start | bytes 65536 | tf_op jit(solution)/shard_map/all_to_all | solution.py:182
  55.4 0.6 copy-start
  62.7 63.3 %copy-start.1 = (bf16[3,1024]{1,0:T(4,128)(2,1)S(1)}, bf16[3,1024]{1,0:T(4,128)(2,1)}, u32[]{:S(2)}) copy-start(bf16[3,1024]{1,0:T(4,128)(2,1)} %param.6) | copy-start | bytes 18436
  62.7 3.8 %collective-permute-start = (f32[8,128]{1,0:T(8,128)}, f32[8,128]{1,0:T(8,128)S(1)}, u32[]{:S(2)}, u32[]{:S(2)}) collective-permute-start(f32[8,128]{1,0:T(8,128)} %get-tuple-element.9.mine_ref), channel_id=1, source_target_pairs={{0,1},{1,0},{2,3},{3,2},{4,5},{5,4},{6,7},{7,6},{8,9},{9,8},{10,11... | collective-permute-start | bytes 12296 | tf_op jit(solution)/shard_map/ppermute | solution.py:203
  66.5 0.6 copy-start.2

commit v2 on v1

v2 whole, which is shorter than its diff:
```python
import math

import jax
import jax.numpy as jnp
import numpy as np
from jax import lax
from jax.experimental import pallas as pl
from jax.experimental.pallas import tpu as pltpu
from jax.sharding import PartitionSpec as P

SIDE = 16
HALF = SIDE // 2
TILE = 128
KT = 12
SLOTS = 16
SLAB = SIDE * SIDE
HERE = HALF * SLAB
F32 = jnp.float32
BF16 = jnp.bfloat16
STEP = 6.0 / 15.0

AXIS = (np.float32(-3.0) + np.float32(6.0) * np.arange(SIDE, dtype=np.float32) / np.float32(15.0)).astype(np.float32)
LOG_TOTAL = 3.0 * math.log(float(np.sum(np.exp(-0.5 * AXIS.astype(np.float64) ** 2))))

VMEM = pl.BlockSpec(memory_space=pltpu.VMEM)
SMEM = pl.BlockSpec(memory_space=pltpu.SMEM)
ANY = pl.BlockSpec(memory_space=pl.ANY)


def params(mib):
    return pltpu.CompilerParams(vmem_limit_bytes=mib << 20)


def axis_column():
    index = lax.broadcasted_iota(jnp.int32, (SIDE, TILE), 0)
    index = jnp.where(index < HALF, index, SIDE + HALF - 1 - index).astype(F32)
    return -3.0 + 6.0 * index / 15.0


def first_theta0(place_ref):
    return -3.0 + STEP * HALF * (place_ref[0] & 1).astype(F32)


def tile_start(par_ref, k, first):
    a0, a1, a2, d, c = (par_ref[j, k : k + 1, :] for j in range(5))
    base = jnp.exp(a2 * axis_column() + (a0 * first + a1 * float(AXIS[0]) + d))
    ratio0 = jnp.broadcast_to(jnp.exp(a0 * STEP), (SIDE, TILE))
    ratio1 = jnp.broadcast_to(jnp.exp(a1 * STEP), (SIDE, TILE))
    return base, ratio0, ratio1, c


def offer_kernel(place_ref, slopes_ref, icpt_ref, guess_ref, out_ref):
    place = place_ref[0]
    slopes = slopes_ref[...].astype(F32)
    row = jnp.where(place == 0, slopes[0:1], jnp.where(place == 1, slopes[1:2], slopes[2:3]))
    rows = jnp.concatenate([row[:, j * TILE : (j + 1) * TILE] for j in range(row.shape[1] // TILE)], axis=0)
    rows = jnp.where(place == 3, icpt_ref[...].astype(F32), rows)
    rows = jnp.where(place >= 4, guess_ref[...].astype(F32), rows)
    out_ref[...] = jnp.broadcast_to(rows.astype(BF16)[None], out_ref.shape)


def marks_kernel(place_ref, count_ref, resp_ref, first_ref, second_ref, buf_ref, sem_ref):
    block = place_ref[0] >> 1
    copies = [pltpu.make_async_copy(resp_ref.at[block, k], buf_ref.at[k], sem_ref.at[k]) for k in range(KT)]
    for copy in copies:
        copy.start()
    count = count_ref[block]
    for k, copy in enumerate(copies):
        copy.wait()
        codes = jnp.where(k < count, buf_ref[k], 0)
        second_ref[k, :, 0:TILE] = (codes == 2).astype(BF16)
        second_ref[k, :, TILE : 2 * TILE] = (codes > 0).astype(BF16)
        turned = jnp.transpose(codes.astype(F32))
        first_ref[2 * k] = (turned == 2.0).astype(BF16)
        first_ref[2 * k + 1] = (turned == 1.0).astype(BF16)


def pick_kernel(items_ref, table_ref, out_ref, wide_ref, rows_ref):
    wide_ref[...] = table_ref[...].astype(F32)
    last = wide_ref.shape[0] - 1
    for b in range(4):
        rows_ref[b, KT:SLOTS, :] = jnp.zeros((SLOTS - KT, TILE), F32)
        for k in range(KT):
            item = jnp.minimum(jnp.maximum(items_ref[b, k], 0), last)
            rows_ref[b, k : k + 1, :] = wide_ref[pl.ds(item, 1), :]
    for b in range(4):
        rows = rows_ref[b].astype(BF16)
        out_ref[2 * b] = rows
        out_ref[2 * b + 1] = rows


def likelihood_kernel(place_ref, got_ref, marks_ref, w_ref, st_ref, par_ref, tab_a, tab_b):
    first = first_theta0(place_ref)
    par_ref[...] = got_ref[...].astype(F32)
    theta2 = axis_column()
    half_square = -0.5 * (theta2 * theta2)
    for j0 in range(HALF):
        theta0 = first + STEP * j0
        for j1 in range(SIDE):
            rows = pl.ds((j0 * SIDE + j1) * SIDE, SIDE)
            w_ref[rows, :] = half_square - (0.5 * (theta0 * theta0) + (0.5 * float(AXIS[j1]) ** 2 + LOG_TOTAL))

    def tables(k, tab_ref, at):
        base, ratio0, ratio1, c = tile_start(par_ref, k, first)
        c_b = jnp.broadcast_to(c, (SIDE, TILE))
        log_rest = jnp.broadcast_to(jnp.log(1.0 - c), (SIDE, TILE))
        for j0 in range(HALF):
            u = base
            for j1 in range(SIDE):
                rows = pl.ds((j0 * SIDE + j1) * SIDE, SIDE)
                log_one = jnp.log(1.0 + u)
                tab_ref[rows, at : at + TILE] = (jnp.log(c_b + u) - log_one).astype(BF16)
                tab_ref[rows, at + TILE : at + 2 * TILE] = (log_rest - log_one).astype(BF16)
                u = u * ratio1
            base = base * ratio0

    def gather(pair, tab_ref):
        marks = marks_ref[pl.ds(4 * pair, 4)].reshape(4 * TILE, TILE)
        for s in range(0, HERE, 2 * SLAB):
            w_ref[s : s + 2 * SLAB, :] += jnp.dot(tab_ref[s : s + 2 * SLAB, :], marks, preferred_element_type=F32)

    for pair in range(KT // 2):
        tab_ref = (tab_a, tab_b)[pair % 2]
        for side in range(2):
            tables(2 * pair + side, tab_ref, 2 * TILE * side)
        if pair:
            gather(pair - 1, (tab_a, tab_b)[1 - pair % 2])
    gather(KT // 2 - 1, (tab_a, tab_b)[(KT // 2 - 1) % 2])

    top = jnp.full((SIDE, TILE), -jnp.inf, F32)
    for j in range(HALF * SIDE):
        top = jnp.maximum(top, w_ref[j * SIDE : (j + 1) * SIDE, :])
    top = jnp.max(top, axis=0, keepdims=True)
    total = jnp.zeros((SIDE, TILE), F32)
    mom0 = jnp.zeros((SIDE, TILE), F32)
    mom1 = jnp.zeros((SIDE, TILE), F32)
    for j0 in range(HALF):
        slab_sum = jnp.zeros((SIDE, TILE), F32)
        for j1 in range(SIDE):
            rows = pl.ds((j0 * SIDE + j1) * SIDE, SIDE)
            w = jnp.exp(w_ref[rows, :] - top)
            w_ref[rows, :] = w
            slab_sum = slab_sum + w
            mom1 = mom1 + float(AXIS[j1]) * w
        total = total + slab_sum
        mom0 = mom0 + (first + STEP * j0) * slab_sum
    st_ref[0:1, :] = top
    for j, part in enumerate((total, mom0, mom1, total * theta2)):
        st_ref[j + 1 : j + 2, :] = jnp.sum(part, axis=0, keepdims=True)
    st_ref[5:8, :] = jnp.zeros((3, TILE), F32)


def statistics_kernel(place_ref, got_ref, marks_ref, w_ref, mine_ref, other_ref, out_ref, par_ref, post_ref):
    first = first_theta0(place_ref)
    par_ref[...] = got_ref[...].astype(F32)
    mine, other = mine_ref[...], other_ref[...]
    top = jnp.maximum(mine[0:1], other[0:1])
    both = mine[1:5] * jnp.exp(mine[0:1] - top) + other[1:5] * jnp.exp(other[0:1] - top)
    log_norm = top + jnp.log(both[0:1])
    means = both[1:4] / both[0:1]
    scale = jnp.exp(mine[0:1] - log_norm)
    post_ref[...] = (w_ref[...] * scale).astype(BF16)
    for j in range(8):
        out_ref[j, KT : KT + 1, :] = log_norm
        out_ref[j, KT + 1 : KT + 4, :] = means
    theta2 = axis_column()
    zero = jnp.zeros((SIDE, TILE), F32)
    zero_h = jnp.zeros((HALF, TILE), F32)

    def tile(k):
        marks = marks_ref[k]
        a0, a1, a2, d, c = (par_ref[j, pl.ds(k, 1), :] for j in range(5))
        base = jnp.exp(a2 * theta2 + (a0 * first + a1 * float(AXIS[0]) + d))
        ratio0 = jnp.broadcast_to(jnp.exp(a0 * STEP), (SIDE, TILE))
        ratio1 = jnp.broadcast_to(jnp.exp(a1 * STEP), (SIDE, TILE))
        c_b = jnp.broadcast_to(c, (SIDE, TILE))
        g_all, g_0, g_run = zero, zero, zero_h
        f_all, f_0, f_1 = zero_h, zero_h, zero_h
        for j0 in range(HALF):
            counts = jnp.dot(post_ref[j0 * SLAB : (j0 + 1) * SLAB, :], marks, preferred_element_type=F32)
            theta0 = first + STEP * j0
            u = base
            g_slab, f_slab = zero, zero_h
            for j1 in range(SIDE):
                hits = counts[j1 * SIDE : (j1 + 1) * SIDE, 0:TILE]
                mass = counts[j1 * SIDE : (j1 + 1) * SIDE, TILE : 2 * TILE]
                miss = 1.0 / (1.0 + u)
                share = u * (1.0 / (c_b + u))
                mass_sig = mass * (u * miss)
                info = mass_sig * (share * miss)
                g_slab = g_slab + (hits * share - mass_sig)
                g_run = g_run + (g_slab[:HALF] + g_slab[HALF:])
                info = info[:HALF] + info[HALF:]
                f_slab = f_slab + info
                f_1 = f_1 + float(AXIS[j1]) ** 2 * info
                u = u * ratio1
            g_all, f_all = g_all + g_slab, f_all + f_slab
            g_0, f_0 = g_0 + theta0 * g_slab, f_0 + (theta0 * theta0) * f_slab
            base = base * ratio0
        square = theta2[:HALF] * theta2[:HALF]
        g_sum = g_all[:HALF] + g_all[HALF:]
        g_1 = (float(AXIS[-1]) + STEP) * g_sum - STEP * g_run
        rest = 1.0 - c
        rows = (g_0, g_1, theta2 * g_all, g_sum, f_0, f_1, square * f_all, f_all)
        for j, part in enumerate(rows):
            summed = jnp.sum(part, axis=0, keepdims=True)
            out_ref[j, pl.ds(k, 1), :] = summed if j < 4 else summed * rest

    @pl.loop(0, KT // 2)
    def _(pair):
        tile(2 * pair)
        tile(2 * pair + 1)


def spread_kernel(items_ref, count_ref, got_ref, out_ref, marg_ref, mean_ref, acc_ref):
    acc_ref[...] = jnp.zeros(acc_ref.shape, F32)
    last = acc_ref.shape[0] - 1
    for b in range(4):
        marg_ref[0:1, b * TILE : (b + 1) * TILE] = got_ref[2 * b, KT : KT + 1, :]
        mean_ref[:, b * TILE : (b + 1) * TILE] = got_ref[2 * b, KT + 1 : KT + 4, :]
        both = got_ref[2 * b] + got_ref[2 * b + 1]
        for k in range(KT):
            row = pl.ds(jnp.minimum(jnp.maximum(items_ref[b, k], 0), last), 1)
            acc_ref[row, :] += both[k : k + 1]
    out_ref[...] = acc_ref[...].astype(BF16)


def gather_kernel(got_ref, out_ref):
    total = jnp.sum(got_ref[...].astype(F32), axis=0)
    out_ref[...] = jnp.broadcast_to(total[None], out_ref.shape)


def shape(dims, kind=F32):
    return jax.ShapeDtypeStruct(dims, kind)


def local(slopes, intercepts, guessing, responses, tile_items, tile_count):
    takers = lax.axis_size("takers")
    place = lax.axis_index("nodes").reshape(1)
    own = slopes.shape[1]
    rows = own // TILE
    blocks = takers * rows
    offer = pl.pallas_call(
        offer_kernel,
        out_shape=shape((takers, rows, TILE), BF16),
        in_specs=[SMEM, VMEM, VMEM, VMEM],
        out_specs=VMEM,
        compiler_params=params(4),
        name="offer",
    )(place, slopes, intercepts.reshape(rows, TILE), guessing.reshape(rows, TILE))
    marks1, marks2 = pl.pallas_call(
        marks_kernel,
        out_shape=(shape((2 * KT, TILE, TILE), BF16), shape((KT, TILE, 2 * TILE), BF16)),
        in_specs=[SMEM, SMEM, ANY],
        out_specs=(VMEM, VMEM),
        scratch_shapes=[pltpu.VMEM((KT, TILE, TILE), jnp.int32), pltpu.SemaphoreType.DMA((KT,))],
        compiler_params=params(6),
        name="marks",
    )(place, tile_count, responses)
    table = lax.all_to_all(offer, "takers", 0, 0).reshape(blocks, TILE)
    picked = pl.pallas_call(
        pick_kernel,
        out_shape=shape((8, SLOTS, TILE), BF16),
        in_specs=[SMEM, VMEM],
        out_specs=VMEM,
        scratch_shapes=[pltpu.VMEM((blocks, TILE), F32), pltpu.VMEM((4, SLOTS, TILE), F32)],
        compiler_params=params(4),
        name="pick",
    )(tile_items, table)
    got = lax.all_to_all(picked, "nodes", 0, 0)
    weights, state = pl.pallas_call(
        likelihood_kernel,
        out_shape=(shape((HERE, TILE)), shape((8, TILE))),
        in_specs=[SMEM, VMEM, VMEM],
        out_specs=(VMEM, VMEM),
        scratch_shapes=[
            pltpu.VMEM((8, SLOTS, TILE), F32),
            pltpu.VMEM((HERE, 4 * TILE), BF16),
            pltpu.VMEM((HERE, 4 * TILE), BF16),
        ],
        compiler_params=params(14),
        name="likelihood",
    )(place, got, marks1)
    other = lax.ppermute(state, "nodes", [(i, i ^ 1) for i in range(8)])
    stats = pl.pallas_call(
        statistics_kernel,
        out_shape=shape((8, SLOTS, TILE)),
        in_specs=[SMEM, VMEM, VMEM, VMEM, VMEM, VMEM],
        out_specs=VMEM,
        scratch_shapes=[pltpu.VMEM((8, SLOTS, TILE), F32), pltpu.VMEM((HERE, TILE), BF16)],
        compiler_params=params(14),
        name="statistics",
    )(place, got, marks2, weights, state, other)
    partial = lax.all_to_all(stats, "nodes", 0, 0)
    spread, marginal, means = pl.pallas_call(
        spread_kernel,
        out_shape=(shape((blocks, TILE), BF16), shape((1, 4 * TILE)), shape((3, 4 * TILE))),
        in_specs=[SMEM, SMEM, VMEM],
        out_specs=(VMEM, VMEM, VMEM),
        scratch_shapes=[pltpu.VMEM((blocks, TILE), F32)],
        compiler_params=params(4),
        name="spread",
    )(tile_items, tile_count, partial)
    owned = lax.all_to_all(spread.reshape(takers, rows, TILE), "takers", 0, 0)
    summed = pl.pallas_call(
        gather_kernel,
        out_shape=shape((8, rows, TILE)),
        in_specs=[VMEM],
        out_specs=VMEM,
        compiler_params=params(4),
        name="gather",
    )(owned)
    all_stats = lax.all_to_all(summed, "nodes", 0, 0).reshape(8, own)
    current = jnp.concatenate([slopes.astype(F32), intercepts.astype(F32)[None]], axis=0)
    new_params = current + all_stats[:4] / (all_stats[4:] + 1.0)
    return new_params, marginal.reshape(-1), means


def solution(mesh):
    in_specs = (
        P(None, "takers"),
        P("takers"),
        P("takers"),
        P("takers", None, None, None),
        P("takers", None),
        P("takers"),
    )
    out_specs = (P(None, "takers"), P("takers"), P(None, "takers"))
    return jax.shard_map(local, mesh=mesh, in_specs=in_specs, out_specs=out_specs, check_vma=False)
```

time: 127 us -> 114 us (0.90)
  starting transfers between devices: 30.1 us -> 16.8 us
  blocking collectives: 49.4 us -> 62.3 us
  waiting for transfers between devices: 17.3 us -> 5.86 us
  Pallas kernels: 16.1 us -> 21.4 us
  other arithmetic: 5.5 us -> 0.63 us
  local copies, waits for them, and re-layouts: 6.72 us -> 5.31 us
    all_to_all x2, blocking collectives: 32.5 us -> 52.9 us  [the longest x1 33.8 us: local(): table = lax.all_to_all(offer, 'takers', 0, 0).reshape(blocks, TILE)]
    all_to_all x1, starting transfers between devices: 19.1 us -> 6.67 us  [local(): all_stats = lax.all_to_all(summed, 'nodes', 0, 0).reshape(8, own)]
    all_to_all x1, waiting for transfers between devices: 12.9 us -> 4.73 us  [local(): all_stats = lax.all_to_all(summed, 'nodes', 0, 0).reshape(8, own)]
    all_to_all x1, blocking collectives: 16.8 us -> 9.45 us  [local(): partial = lax.all_to_all(stats, 'nodes', 0, 0)]
    pallas_call x3 -> x7, Pallas kernels: 16.1 us -> 21.4 us  [the longest x1 7.73 us: local(): pl.pallas_call(statistics_kernel, out_shape=shape((8, SLOTS, TILE)), in_s...]
    all_to_all x1, waiting for transfers between devices: 3.43 us -> 0.01 us  [local(): got = lax.all_to_all(picked, 'nodes', 0, 0)]
    unnamed x8 -> x20, local copies, waits for them, and re-layouts: 2.01 us -> 5.31 us
    dynamic_slice x2 -> x0, local copies, waits for them, and re-layouts: 1.83 us -> none  [the longest x1 1.24 us: local(): scalars = jnp.stack([block, tile_count[block], core])]
  transfers between devices with their start and end apart: 3 -> 3, of which waited for: 3 -> 2; matrix products, arithmetic and copies ran while one was open for 3% -> 0% of each run, Pallas kernels for 0% -> 3%
where the time goes in v2:
time: 114 us; the launch traced here: 113 us
  blocking collectives  62.3 us (55%)
  Pallas kernels  21.4 us (19%)
  starting transfers between devices  16.8 us (15%)
  waiting for transfers between devices  5.86 us (5%)
  local copies, waits for them, and re-layouts  5.31 us (5%)
    all_to_all x1, blocking collectives, local(): table = lax.all_to_all(offer, 'takers', 0, 0).reshape(blocks, TILE)  33.8 us
    all_to_all x1, blocking collectives, local(): owned = lax.all_to_all(spread.reshape(takers, rows, TILE), 'takers', 0, 0)  19.1 us
    all_to_all x1, blocking collectives, local(): partial = lax.all_to_all(stats, 'nodes', 0, 0)  9.45 us
    all_to_all x1, starting transfers between devices, local(): got = lax.all_to_all(picked, 'nodes', 0, 0)  8.2 us
    pallas_call x1, Pallas kernels, local(): pl.pallas_call(statistics_kernel, out_shape=shape((8, SLOTS, TILE)), in_s...  7.73 us
    pallas_call x1, Pallas kernels, local(): pl.pallas_call(likelihood_kernel, out_shape=(shape((HERE, TILE)), shape((...  7.46 us
    all_to_all x1, starting transfers between devices, local(): all_stats = lax.all_to_all(summed, 'nodes', 0, 0).reshape(8, own)  6.67 us
    unnamed x20, local copies, waits for them, and re-layouts  5.31 us
  transfers between devices with their start and end apart: 3, of which 2 were waited for; matrix products, arithmetic and copies ran while one was open for 0% of the time, Pallas kernels for 3%

profile of v2, /device:TPU:1, one launch (start us, length us, event | category | flops | bytes accessed | tf_op | source)
XLA Modules:
  0.0 113.0 jit_solution(4460038033423139384)
XLA Ops:
  0.6 0.0 copy-start.1
  0.6 0.7 copy-done.1
  1.3 0.7 copy-done.3
  2.0 0.7 copy-done.7
  2.7 33.8 %all_to_all.25 = bf16[64,8,128]{2,1,0:T(8,128)(2,1)S(1)} all-to-all(bf16[64,8,128]{2,1,0:T(8,128)(2,1)S(1)} %offer.1), channel_id=1, replica_groups=mesh['takers'=64,'nodes'=8] {'takers'}, dimensions={0} | all-to-all | bytes 262144 | tf_op jit(solution)/shard_map/all_to_all | solution.py:260
  36.5 0.7 copy-done.5
  37.2 1.3 %pick.1 = bf16[8,16,128]{2,1,0:T(8,128)(2,1)} custom-call(s32[4,12]{1,0:T(4,128)S(1)} %copy-done.5, bf16[512,128]{1,0:T(8,128)(2,1)S(1)} %bitcast.10), custom_call_target="tpu_custom_call" | custom-call | tf_op jit(solution)/shard_map/pick/pallas_call | solution.py:261
  38.5 8.2 %all-to-all-start.1 = ((bf16[8,16,128]{2,1,0:T(8,128)(2,1)}), bf16[8,16,128]{2,1,0:T(8,128)(2,1)S(1)}, u32[]{:S(2)}, u32[]{:S(2)}) async-start(bf16[8,16,128]{2,1,0:T(8,128)(2,1)} %pick.1), calls=%async_computation.1 | async-start | bytes 65536 | tf_op jit(solution)/shard_map/all_to_all | solution.py:270
  46.7 1.9 %copy-done = s32[4,12,128,128]{3,2,1,0:T(8,128)S(1)} copy-done((s32[4,12,128,128]{3,2,1,0:T(8,128)S(1)}, s32[4,12,128,128]{3,2,1,0:T(8,128)}, u32[]{:S(2)}) %copy-start) | copy-done | bytes 3145752
  48.6 0.7 copy-done.8
  49.3 2.9 %marks.1 = (bf16[24,128,128]{2,1,0:T(8,128)(2,1)S(1)}, bf16[12,128,256]{2,1,0:T(8,128)(2,1)S(1)}) custom-call(s32[1]{0:T(128)} %bitcast.place_ref, s32[4]{0:T(128)S(1)} %copy-done.8, s32[4,12,128,128]{3,2,1,0:T(8,128)S(1)} %copy-done), custom_call_target="tpu_custom_call" | custom-call | tf_op jit(solution)/shard_map/marks/pallas_call | solution.py:251
  52.2 0.0 all-to-all-done.1.got_ref
  52.2 7.5 %likelihood.1 = (f32[2048,128]{1,0:T(8,128)S(1)}, f32[8,128]{1,0:T(8,128)S(1)}) custom-call(s32[1]{0:T(128)} %bitcast.place_ref, bf16[8,16,128]{2,1,0:T(8,128)(2,1)S(1)} %all-to-all-done.1.got_ref, bf16[24,128,128]{2,1,0:T(8,128)(2,1)S(1)} %get-tuple-element.11.marks_ref), custom_call_target="tpu_custom_call" | custom-call | tf_op jit(solution)/shard_map/likelihood/pallas_call | solution.py:271
  59.7 1.9 %collective-permute-start = (f32[8,128]{1,0:T(8,128)S(1)}, f32[8,128]{1,0:T(8,128)S(1)}, u32[]{:S(2)}, u32[]{:S(2)}) collective-permute-start(f32[8,128]{1,0:T(8,128)S(1)} %get-tuple-element.13.mine_ref), channel_id=1, source_target_pairs={{0,1},{1,0},{2,3},{3,2},{4,5},{5,4},{6,7},{7,6},{8,9},{9,8},{10,11... | collective-permute-start | bytes 12296 | tf_op jit(solution)/shard_map/ppermute | solution.py:284
  61.6 1.1 %collective-permute-done.other_ref = f32[8,128]{1,0:T(8,128)S(1)} collective-permute-done((f32[8,128]{1,0:T(8,128)S(1)}, f32[8,128]{1,0:T(8,128)S(1)}, u32[]{:S(2)}, u32[]{:S(2)}) %collective-permute-start) | collective-permute-done | bytes 4128 | tf_op jit(solution)/shard_map/ppermute | solution.py:284
  62.7 7.7 %statistics.1 = f32[8,16,128]{2,1,0:T(8,128)S(1)} custom-call(s32[1]{0:T(128)} %bitcast.place_ref, bf16[8,16,128]{2,1,0:T(8,128)(2,1)S(1)} %all-to-all-done.1.got_ref, bf16[12,128,256]{2,1,0:T(8,128)(2,1)S(1)} %get-tuple-element.10.marks_ref, f32[2048,128]{1,0:T(8,128)S(1)} %get-tuple-element.12.w_ref, f32[8,128]{1,0:T(8,128)S(1)} %get-tuple-element.13.mine_ref, ...), custom_call_target="tpu_custom_call" | custom-call | tf_op jit(solution)/shard_map/statistics/pallas_call | solution.py:285
  70.5 9.5 %all_to_all.26.got_ref = f32[8,16,128]{2,1,0:T(8,128)S(1)} all-to-all(f32[8,16,128]{2,1,0:T(8,128)S(1)} %statistics.1), channel_id=1, replica_groups=mesh['takers'=64,'nodes'=8] {'nodes'}, dimensions={0} | all-to-all | bytes 131072 | tf_op jit(solution)/shard_map/all_to_all | solution.py:294
  79.9 0.0 copy-done.9
  79.9 1.3 %spread.1 = (bf16[512,128]{1,0:T(8,128)(2,1)S(1)}, f32[1,512]{1,0:T(1,128)}, f32[3,512]{1,0:T(4,128)}) custom-call(s32[4,12]{1,0:T(4,128)S(1)} %copy-done.6, s32[4]{0:T(128)S(1)} %copy-done.9, f32[8,16,128]{2,1,0:T(8,128)S(1)} %all_to_all.26.got_ref), custom_call_target="tpu_custom_call" | custom-call | tf_op jit(solution)/shard_map/spread/pallas_call | solution.py:295
  81.2 19.1 %all_to_all.27.got_ref = bf16[64,8,128]{2,1,0:T(8,128)(2,1)S(1)} all-to-all(bf16[64,8,128]{2,1,0:T(8,128)(2,1)S(1)} %bitcast.11), channel_id=1, replica_groups=mesh['takers'=64,'nodes'=8] {'takers'}, dimensions={0} | all-to-all | bytes 262144 | tf_op jit(solution)/shard_map/all_to_all | solution.py:304
  100.3 0.7 gather.1
  101.0 6.7 %all-to-all-start.4 = ((f32[8,8,128]{2,1,0:T(8,128)}), f32[8,8,128]{2,1,0:T(8,128)S(1)}, u32[]{:S(2)}, u32[]{:S(2)}) async-start(f32[8,8,128]{2,1,0:T(8,128)} %gather.1), calls=%async_computation.4 | async-start | bytes 65536 | tf_op jit(solution)/shard_map/all_to_all | solution.py:313
  107.7 4.7 %all-to-all-done.4 = f32[8,8,128]{2,1,0:T(8,128)S(1)} async-done(((f32[8,8,128]{2,1,0:T(8,128)}), f32[8,8,128]{2,1,0:T(8,128)S(1)}, u32[]{:S(2)}, u32[]{:S(2)}) %all-to-all-start.4) | async-done | bytes 32800 | tf_op jit(solution)/shard_map/all_to_all | solution.py:313
  112.4 0.6 bitcast_add_fusion
  (15 shorter events, 0.1 us)
Async XLA Ops:
  0.6 0.7 copy-start.1
  1.3 0.7 copy-start.3
  2.0 0.7 copy-start.7
  36.5 43.4 %copy-start.9 = (s32[4]{0:T(128)S(1)}, s32[4]{0:T(128)}, u32[]{:S(2)}) copy-start(s32[4]{0:T(128)} %count_ref.3) | copy-start | bytes 52
  36.5 0.7 copy-start.5
  37.2 42.7 %copy-start.6 = (s32[4,12]{1,0:T(4,128)S(1)}, s32[4,12]{1,0:T(4,128)}, u32[]{:S(2)}) copy-start(s32[4,12]{1,0:T(4,128)} %items_ref.3) | copy-start | bytes 580
  38.5 13.7 %all-to-all-start.1 = ((bf16[8,16,128]{2,1,0:T(8,128)(2,1)}), bf16[8,16,128]{2,1,0:T(8,128)(2,1)S(1)}, u32[]{:S(2)}, u32[]{:S(2)}) async-start(bf16[8,16,128]{2,1,0:T(8,128)(2,1)} %pick.1), calls=%async_computation.1 | async-start | bytes 65536 | tf_op jit(solution)/shard_map/all_to_all | solution.py:270
  46.7 1.9 %copy-start = (s32[4,12,128,128]{3,2,1,0:T(8,128)S(1)}, s32[4,12,128,128]{3,2,1,0:T(8,128)}, u32[]{:S(2)}) copy-start(s32[4,12,128,128]{3,2,1,0:T(8,128)} %resp_ref.1) | copy-start | bytes 9437188
  48.6 0.7 copy-start.8
  49.2 58.4 %copy-start.4 = (bf16[1024]{0:T(1024)(128)(2,1)S(1)}, bf16[1024]{0:T(1024)(128)(2,1)}, u32[]{:S(2)}) copy-start(bf16[1024]{0:T(1024)(128)(2,1)} %param.7) | copy-start | bytes 6148
  49.2 63.1 %copy-start.2 = (bf16[3,1024]{1,0:T(4,128)(2,1)S(1)}, bf16[3,1024]{1,0:T(4,128)(2,1)}, u32[]{:S(2)}) copy-start(bf16[3,1024]{1,0:T(4,128)(2,1)} %slopes_ref.1) | copy-start | bytes 18436
  59.7 3.1 %collective-permute-start = (f32[8,128]{1,0:T(8,128)S(1)}, f32[8,128]{1,0:T(8,128)S(1)}, u32[]{:S(2)}, u32[]{:S(2)}) collective-permute-start(f32[8,128]{1,0:T(8,128)S(1)} %get-tuple-element.13.mine_ref), channel_id=1, source_target_pairs={{0,1},{1,0},{2,3},{3,2},{4,5},{5,4},{6,7},{7,6},{8,9},{9,8},{10,11... | collective-permute-start | bytes 12296 | tf_op jit(solution)/shard_map/ppermute | solution.py:284
  101.0 11.4 %all-to-all-start.4 = ((f32[8,8,128]{2,1,0:T(8,128)}), f32[8,8,128]{2,1,0:T(8,128)S(1)}, u32[]{:S(2)}, u32[]{:S(2)}) async-start(f32[8,8,128]{2,1,0:T(8,128)} %gather.1), calls=%async_computation.4 | async-start | bytes 65536 | tf_op jit(solution)/shard_map/all_to_all | solution.py:313

commit v3 on v2

--- a/solution.py
+++ b/solution.py
@@ -24,7 +24,7 @@
 
 VMEM = pl.BlockSpec(memory_space=pltpu.VMEM)
 SMEM = pl.BlockSpec(memory_space=pltpu.SMEM)
-ANY = pl.BlockSpec(memory_space=pl.ANY)
+HBM = pl.BlockSpec(memory_space=pltpu.HBM)
 
 
 def params(mib):
@@ -42,14 +42,23 @@
 
 
 def tile_start(par_ref, k, first):
-    a0, a1, a2, d, c = (par_ref[j, k : k + 1, :] for j in range(5))
+    a0, a1, a2, d, c = (par_ref[j, pl.ds(k, 1), :] for j in range(5))
     base = jnp.exp(a2 * axis_column() + (a0 * first + a1 * float(AXIS[0]) + d))
     ratio0 = jnp.broadcast_to(jnp.exp(a0 * STEP), (SIDE, TILE))
     ratio1 = jnp.broadcast_to(jnp.exp(a1 * STEP), (SIDE, TILE))
     return base, ratio0, ratio1, c
 
 
-def offer_kernel(place_ref, slopes_ref, icpt_ref, guess_ref, out_ref):
+def offer_kernel(place_ref, slopes_hbm, icpt_hbm, guess_hbm, out_ref, slopes_ref, icpt_ref, guess_ref, sem_ref):
+    copies = [
+        pltpu.make_async_copy(slopes_hbm, slopes_ref, sem_ref.at[0]),
+        pltpu.make_async_copy(icpt_hbm, icpt_ref, sem_ref.at[1]),
+        pltpu.make_async_copy(guess_hbm, guess_ref, sem_ref.at[2]),
+    ]
+    for copy in copies:
+        copy.start()
+    for copy in copies:
+        copy.wait()
     place = place_ref[0]
     slopes = slopes_ref[...].astype(F32)
     row = jnp.where(place == 0, slopes[0:1], jnp.where(place == 1, slopes[1:2], slopes[2:3]))
@@ -59,37 +68,31 @@
     out_ref[...] = jnp.broadcast_to(rows.astype(BF16)[None], out_ref.shape)
 
 
-def marks_kernel(place_ref, count_ref, resp_ref, first_ref, second_ref, buf_ref, sem_ref):
-    block = place_ref[0] >> 1
-    copies = [pltpu.make_async_copy(resp_ref.at[block, k], buf_ref.at[k], sem_ref.at[k]) for k in range(KT)]
-    for copy in copies:
-        copy.start()
-    count = count_ref[block]
-    for k, copy in enumerate(copies):
-        copy.wait()
-        codes = jnp.where(k < count, buf_ref[k], 0)
-        second_ref[k, :, 0:TILE] = (codes == 2).astype(BF16)
-        second_ref[k, :, TILE : 2 * TILE] = (codes > 0).astype(BF16)
-        turned = jnp.transpose(codes.astype(F32))
-        first_ref[2 * k] = (turned == 2.0).astype(BF16)
-        first_ref[2 * k + 1] = (turned == 1.0).astype(BF16)
-
-
-def pick_kernel(items_ref, table_ref, out_ref, wide_ref, rows_ref):
-    wide_ref[...] = table_ref[...].astype(F32)
-    last = wide_ref.shape[0] - 1
+def plan_kernel(count_ref, items_ref, pick_ref, turn_ref, wide_ref):
+    wide_ref[...] = jnp.zeros(wide_ref.shape, F32)
+    blocks = wide_ref.shape[1]
+    block_of = lax.broadcasted_iota(jnp.int32, (1, blocks), 1)
     for b in range(4):
-        rows_ref[b, KT:SLOTS, :] = jnp.zeros((SLOTS - KT, TILE), F32)
         for k in range(KT):
-            item = jnp.minimum(jnp.maximum(items_ref[b, k], 0), last)
-            rows_ref[b, k : k + 1, :] = wide_ref[pl.ds(item, 1), :]
+            at = b * SLOTS + k
+            wide_ref[at : at + 1, :] = (block_of == items_ref[b, k]).astype(F32)
+            at += 4 * SLOTS
+            wide_ref[at : at + 1, 0:TILE] = jnp.full((1, TILE), k < count_ref[b]).astype(F32)
+    pick_ref[...] = wide_ref[...].astype(BF16)
+    for j in range(blocks // TILE):
+        turn_ref[j * TILE : (j + 1) * TILE, :] = jnp.transpose(wide_ref[:, j * TILE : (j + 1) * TILE]).astype(BF16)
+
+
+def pick_kernel(place_ref, block_ref, pick_ref, table_ref, out_ref):
+    rows = jnp.dot(pick_ref[0 : 4 * SLOTS, :], table_ref[...], preferred_element_type=F32)
+    live = pick_ref[4 * SLOTS : 8 * SLOTS, 0:TILE].astype(F32)
+    rows = jnp.where(place_ref[0] == 5, live, rows).astype(BF16)
     for b in range(4):
-        rows = rows_ref[b].astype(BF16)
-        out_ref[2 * b] = rows
-        out_ref[2 * b + 1] = rows
-
-
-def likelihood_kernel(place_ref, got_ref, marks_ref, w_ref, st_ref, par_ref, tab_a, tab_b):
+        out_ref[2 * b] = rows[b * SLOTS : (b + 1) * SLOTS]
+        out_ref[2 * b + 1] = rows[b * SLOTS : (b + 1) * SLOTS]
+
+
+def likelihood_kernel(place_ref, got_ref, resp_ref, w_ref, st_ref, par_ref, tab_a, tab_b, mark_a, mark_b):
     first = first_theta0(place_ref)
     par_ref[...] = got_ref[...].astype(F32)
     theta2 = axis_column()
@@ -114,18 +117,30 @@
                 u = u * ratio1
             base = base * ratio0
 
-    def gather(pair, tab_ref):
-        marks = marks_ref[pl.ds(4 * pair, 4)].reshape(4 * TILE, TILE)
-        for s in range(0, HERE, 2 * SLAB):
-            w_ref[s : s + 2 * SLAB, :] += jnp.dot(tab_ref[s : s + 2 * SLAB, :], marks, preferred_element_type=F32)
-
-    for pair in range(KT // 2):
-        tab_ref = (tab_a, tab_b)[pair % 2]
-        for side in range(2):
-            tables(2 * pair + side, tab_ref, 2 * TILE * side)
-        if pair:
-            gather(pair - 1, (tab_a, tab_b)[1 - pair % 2])
-    gather(KT // 2 - 1, (tab_a, tab_b)[(KT // 2 - 1) % 2])
+    def mark(k, mark_ref, at):
+        codes = jnp.transpose(resp_ref[k].astype(F32))
+        live = par_ref[5, pl.ds(k, 1), :]
+        mark_ref[at : at + TILE, :] = jnp.where(codes == 2.0, live, 0.0).astype(BF16)
+        mark_ref[at + TILE : at + 2 * TILE, :] = jnp.where(codes == 1.0, live, 0.0).astype(BF16)
+
+    def gather(tab_ref, mark_ref):
+        marks = mark_ref[...]
+        for s in range(0, HERE, 4 * SLAB):
+            w_ref[s : s + 4 * SLAB, :] += jnp.dot(tab_ref[s : s + 4 * SLAB, :], marks, preferred_element_type=F32)
+
+    def both(step, carry):
+        for half, (tab_ref, mark_ref) in enumerate(((tab_a, mark_a), (tab_b, mark_b))):
+            for side in range(2):
+                k = 4 * step + 2 * half + side
+                mark(k, mark_ref, 2 * TILE * side)
+                tables(k, tab_ref, 2 * TILE * side)
+            gather(*((tab_b, mark_b), (tab_a, mark_a))[half])
+        return carry
+
+    tab_b[...] = jnp.zeros(tab_b.shape, BF16)
+    mark_b[...] = jnp.zeros(mark_b.shape, BF16)
+    lax.fori_loop(0, KT // 4, both, 0)
+    gather(tab_b, mark_b)
 
     top = jnp.full((SIDE, TILE), -jnp.inf, F32)
     for j in range(HALF * SIDE):
@@ -150,7 +165,7 @@
     st_ref[5:8, :] = jnp.zeros((3, TILE), F32)
 
 
-def statistics_kernel(place_ref, got_ref, marks_ref, w_ref, mine_ref, other_ref, out_ref, par_ref, post_ref):
+def statistics_kernel(place_ref, got_ref, resp_ref, w_ref, mine_ref, other_ref, out_ref, par_ref, post_ref):
     first = first_theta0(place_ref)
     par_ref[...] = got_ref[...].astype(F32)
     mine, other = mine_ref[...], other_ref[...]
@@ -168,8 +183,10 @@
     zero_h = jnp.zeros((HALF, TILE), F32)
 
     def tile(k):
-        marks = marks_ref[k]
-        a0, a1, a2, d, c = (par_ref[j, pl.ds(k, 1), :] for j in range(5))
+        a0, a1, a2, d, c, live = (par_ref[j, pl.ds(k, 1), :] for j in range(6))
+        codes = resp_ref[k]
+        hit, any_answer = jnp.where(codes == 2, live, 0.0), jnp.where(codes > 0, live, 0.0)
+        marks = jnp.concatenate([hit.astype(BF16), any_answer.astype(BF16)], axis=1)
         base = jnp.exp(a2 * theta2 + (a0 * first + a1 * float(AXIS[0]) + d))
         ratio0 = jnp.broadcast_to(jnp.exp(a0 * STEP), (SIDE, TILE))
         ratio1 = jnp.broadcast_to(jnp.exp(a1 * STEP), (SIDE, TILE))
@@ -206,23 +223,25 @@
             summed = jnp.sum(part, axis=0, keepdims=True)
             out_ref[j, pl.ds(k, 1), :] = summed if j < 4 else summed * rest
 
-    @pl.loop(0, KT // 2)
-    def _(pair):
-        tile(2 * pair)
-        tile(2 * pair + 1)
-
-
-def spread_kernel(items_ref, count_ref, got_ref, out_ref, marg_ref, mean_ref, acc_ref):
-    acc_ref[...] = jnp.zeros(acc_ref.shape, F32)
-    last = acc_ref.shape[0] - 1
+    @pl.loop(0, KT // 4)
+    def _(step):
+        for side in range(4):
+            tile(4 * step + side)
+
+
+def spread_kernel(turn_ref, got_ref, out_ref, marg_ref, mean_ref):
+    both = []
     for b in range(4):
         marg_ref[0:1, b * TILE : (b + 1) * TILE] = got_ref[2 * b, KT : KT + 1, :]
         mean_ref[:, b * TILE : (b + 1) * TILE] = got_ref[2 * b, KT + 1 : KT + 4, :]
-        both = got_ref[2 * b] + got_ref[2 * b + 1]
-        for k in range(KT):
-            row = pl.ds(jnp.minimum(jnp.maximum(items_ref[b, k], 0), last), 1)
-            acc_ref[row, :] += both[k : k + 1]
-    out_ref[...] = acc_ref[...].astype(BF16)
+        both.append(got_ref[2 * b] + got_ref[2 * b + 1])
+    both.extend([jnp.zeros((4 * SLOTS, TILE), F32)])
+    both = jnp.concatenate(both, axis=0)
+    high = both.astype(BF16)
+    low = (both - high.astype(F32)).astype(BF16)
+    turn = turn_ref[...]
+    total = jnp.dot(turn, high, preferred_element_type=F32) + jnp.dot(turn, low, preferred_element_type=F32)
+    out_ref[...] = total.astype(BF16)
 
 
 def gather_kernel(got_ref, out_ref):
@@ -230,6 +249,17 @@
     out_ref[...] = jnp.broadcast_to(total[None], out_ref.shape)
 
 
+def update_kernel(slopes_ref, icpt_ref, got_ref, out_ref):
+    slopes = slopes_ref[...].astype(F32)
+    icpt = icpt_ref[...].astype(F32)
+    for p in range(4):
+        step = got_ref[p] / (got_ref[p + 4] + 1.0)
+        for j in range(step.shape[0]):
+            span = slice(j * TILE, (j + 1) * TILE)
+            now = slopes[p : p + 1, span] if p < 3 else icpt[j : j + 1]
+            out_ref[p : p + 1, span] = now + step[j : j + 1]
+
+
 def shape(dims, kind=F32):
     return jax.ShapeDtypeStruct(dims, kind)
 
@@ -237,37 +267,45 @@
 def local(slopes, intercepts, guessing, responses, tile_items, tile_count):
     takers = lax.axis_size("takers")
     place = lax.axis_index("nodes").reshape(1)
+    block = place >> 1
     own = slopes.shape[1]
     rows = own // TILE
     blocks = takers * rows
+    icpt, guess = intercepts.reshape(rows, TILE), guessing.reshape(rows, TILE)
     offer = pl.pallas_call(
         offer_kernel,
         out_shape=shape((takers, rows, TILE), BF16),
-        in_specs=[SMEM, VMEM, VMEM, VMEM],
-        out_specs=VMEM,
-        compiler_params=params(4),
+        in_specs=[SMEM, HBM, HBM, HBM],
+        out_specs=VMEM,
+        scratch_shapes=[
+            pltpu.VMEM((3, own), BF16),
+            pltpu.VMEM((rows, TILE), BF16),
+            pltpu.VMEM((rows, TILE), BF16),
+            pltpu.SemaphoreType.DMA((3,)),
+        ],
+        compiler_params=params(60),
         name="offer",
-    )(place, slopes, intercepts.reshape(rows, TILE), guessing.reshape(rows, TILE))
-    marks1, marks2 = pl.pallas_call(
-        marks_kernel,
-        out_shape=(shape((2 * KT, TILE, TILE), BF16), shape((KT, TILE, 2 * TILE), BF16)),
-        in_specs=[SMEM, SMEM, ANY],
+    )(place, slopes, icpt, guess)
+    pick, turn = pl.pallas_call(
+        plan_kernel,
+        out_shape=(shape((TILE, blocks), BF16), shape((blocks, TILE), BF16)),
+        in_specs=[SMEM, SMEM],
         out_specs=(VMEM, VMEM),
-        scratch_shapes=[pltpu.VMEM((KT, TILE, TILE), jnp.int32), pltpu.SemaphoreType.DMA((KT,))],
+        scratch_shapes=[pltpu.VMEM((TILE, blocks), F32)],
         compiler_params=params(6),
-        name="marks",
-    )(place, tile_count, responses)
+        name="plan",
+    )(tile_count, tile_items)
     table = lax.all_to_all(offer, "takers", 0, 0).reshape(blocks, TILE)
     picked = pl.pallas_call(
         pick_kernel,
         out_shape=shape((8, SLOTS, TILE), BF16),
-        in_specs=[SMEM, VMEM],
-        out_specs=VMEM,
-        scratch_shapes=[pltpu.VMEM((blocks, TILE), F32), pltpu.VMEM((4, SLOTS, TILE), F32)],
+        in_specs=[SMEM, SMEM, VMEM, VMEM],
+        out_specs=VMEM,
         compiler_params=params(4),
         name="pick",
-    )(tile_items, table)
-    got = lax.all_to_all(picked, "nodes", 0, 0)
+    )(place, block, pick, table)
+    got, block = lax.optimization_barrier((lax.all_to_all(picked, "nodes", 0, 0), block))
+    answers = lax.dynamic_index_in_dim(responses, block[0], 0, keepdims=False)
     weights, state = pl.pallas_call(
         likelihood_kernel,
         out_shape=(shape((HERE, TILE)), shape((8, TILE))),
@@ -277,10 +315,12 @@
             pltpu.VMEM((8, SLOTS, TILE), F32),
             pltpu.VMEM((HERE, 4 * TILE), BF16),
             pltpu.VMEM((HERE, 4 * TILE), BF16),
+            pltpu.VMEM((4 * TILE, TILE), BF16),
+            pltpu.VMEM((4 * TILE, TILE), BF16),
         ],
         compiler_params=params(14),
         name="likelihood",
-    )(place, got, marks1)
+    )(place, got, answers)
     other = lax.ppermute(state, "nodes", [(i, i ^ 1) for i in range(8)])
     stats = pl.pallas_call(
         statistics_kernel,
@@ -290,17 +330,16 @@
         scratch_shapes=[pltpu.VMEM((8, SLOTS, TILE), F32), pltpu.VMEM((HERE, TILE), BF16)],
         compiler_params=params(14),
         name="statistics",
-    )(place, got, marks2, weights, state, other)
+    )(place, got, answers, weights, state, other)
     partial = lax.all_to_all(stats, "nodes", 0, 0)
     spread, marginal, means = pl.pallas_call(
         spread_kernel,
         out_shape=(shape((blocks, TILE), BF16), shape((1, 4 * TILE)), shape((3, 4 * TILE))),
-        in_specs=[SMEM, SMEM, VMEM],
+        in_specs=[VMEM, VMEM],
         out_specs=(VMEM, VMEM, VMEM),
-        scratch_shapes=[pltpu.VMEM((blocks, TILE), F32)],
         compiler_params=params(4),
         name="spread",
-    )(tile_items, tile_count, partial)
+    )(turn, partial)
     owned = lax.all_to_all(spread.reshape(takers, rows, TILE), "takers", 0, 0)
     summed = pl.pallas_call(
         gather_kernel,
@@ -310,9 +349,14 @@
         compiler_params=params(4),
         name="gather",
     )(owned)
-    all_stats = lax.all_to_all(summed, "nodes", 0, 0).reshape(8, own)
-    current = jnp.concatenate([slopes.astype(F32), intercepts.astype(F32)[None]], axis=0)
-    new_params = current + all_stats[:4] / (all_stats[4:] + 1.0)
+    new_params = pl.pallas_call(
+        update_kernel,
+        out_shape=shape((4, own)),
+        in_specs=[VMEM, VMEM, VMEM],
+        out_specs=VMEM,
+        compiler_params=params(4),
+        name="update",
+    )(slopes, icpt, lax.all_to_all(summed, "nodes", 0, 0))
     return new_params, marginal.reshape(-1), means
 
 

time: 114 us -> 107 us (0.939)
  blocking collectives: 62.3 us -> 49.9 us
  waiting for transfers between devices: 5.86 us -> 13.6 us
  starting transfers between devices: 16.8 us -> 21.8 us
  local copies, waits for them, and re-layouts: 5.31 us -> 1.4 us
  Pallas kernels: 21.4 us -> 18.9 us
    all_to_all x1 -> x2, blocking collectives: 33.8 us -> 23.2 us  [the longest x1 12.7 us: local(): lax.all_to_all(picked, 'nodes', 0, 0)]
    all_to_all x2 -> x1, waiting for transfers between devices: 4.73 us -> 12.8 us  [local(): table = lax.all_to_all(offer, 'takers', 0, 0).reshape(blocks, TILE)]
    all_to_all x2 -> x1, starting transfers between devices: 14.9 us -> 19.1 us  [local(): table = lax.all_to_all(offer, 'takers', 0, 0).reshape(blocks, TILE)]
    unnamed x20 -> x10, local copies, waits for them, and re-layouts: 5.31 us -> 1.35 us
    all_to_all x1, blocking collectives: 9.45 us -> 7.57 us  [local(): partial = lax.all_to_all(stats, 'nodes', 0, 0)]
    pallas_call x1, Pallas kernels: 0.02 us -> 1.55 us  [local(): pl.pallas_call(offer_kernel, out_shape=shape((takers, rows, TILE), BF16),...]
    pallas_call x1 -> x2, Pallas kernels: 2.92 us -> 1.41 us  [the longest x1 0.79 us: local(): pl.pallas_call(plan_kernel, out_shape=(shape((TILE, blocks), BF16), shape...]
  transfers between devices with their start and end apart: 3 -> 2, of which waited for: 2 -> 2; matrix products, arithmetic and copies ran while one was open for 0% -> 0% of each run, Pallas kernels for 3% -> 1%
where the time goes in v3:
time: 107 us; the launch traced here: 106 us
  blocking collectives  49.9 us (47%)
  starting transfers between devices  21.8 us (20%)
  Pallas kernels  18.9 us (18%)
  waiting for transfers between devices  13.6 us (13%)
  local copies, waits for them, and re-layouts  1.4 us (1%)
    all_to_all x1, starting transfers between devices, local(): table = lax.all_to_all(offer, 'takers', 0, 0).reshape(blocks, TILE)  19.1 us
    all_to_all x1, blocking collectives, local(): owned = lax.all_to_all(spread.reshape(takers, rows, TILE), 'takers', 0, 0)  19.1 us
    all_to_all x1, waiting for transfers between devices, local(): table = lax.all_to_all(offer, 'takers', 0, 0).reshape(blocks, TILE)  12.8 us
    all_to_all x1, blocking collectives, local(): lax.all_to_all(picked, 'nodes', 0, 0)  12.7 us
    all_to_all x1, blocking collectives, local(): lax.all_to_all(summed, 'nodes', 0, 0)  10.5 us
    pallas_call x1, Pallas kernels, local(): pl.pallas_call(statistics_kernel, out_shape=shape((8, SLOTS, TILE)), in_s...  7.72 us
    all_to_all x1, blocking collectives, local(): partial = lax.all_to_all(stats, 'nodes', 0, 0)  7.57 us
    pallas_call x1, Pallas kernels, local(): pl.pallas_call(likelihood_kernel, out_shape=(shape((HERE, TILE)), shape((...  7.33 us
  transfers between devices with their start and end apart: 2, of which 2 were waited for; matrix products, arithmetic and copies ran while one was open for 0% of the time, Pallas kernels for 1%

profile of v3, /device:TPU:1, one launch (start us, length us, event | category | flops | bytes accessed | tf_op | source)
XLA Modules:
  0.0 106.2 jit_solution(2564328008841539981)
XLA Ops:
  0.6 0.0 copy-start
  0.6 0.0 copy-start.1
  0.7 0.0 copy-start.2
  0.7 1.6 %offer.1 = bf16[64,8,128]{2,1,0:T(8,128)(2,1)} custom-call(s32[1]{0:T(128)} %bitcast.1.place_ref, bf16[3,1024]{1,0:T(4,128)(2,1)} %slopes_ref.1, bf16[8,128]{1,0:T(8,128)(2,1)} %bitcast.11, bf16[8,128]{1,0:T(8,128)(2,1)} %bitcast.13), custom_call_target="tpu_custom_call" | custom-call | tf_op jit(solution)/shard_map/offer/pallas_call | solution.py:275
  2.2 19.1 %all-to-all-start = ((bf16[64,8,128]{2,1,0:T(8,128)(2,1)}), bf16[64,8,128]{2,1,0:T(8,128)(2,1)S(1)}, u32[]{:S(2)}, u32[]{:S(2)}) async-start(bf16[64,8,128]{2,1,0:T(8,128)(2,1)} %offer.1), calls=%async_computation | async-start | bytes 262144 | tf_op jit(solution)/shard_map/all_to_all | solution.py:298
  21.4 0.0 copy-start.3
  21.4 0.7 copy-done.3
  22.0 0.7 copy-done.4
  22.7 0.8 plan.1
  23.5 12.8 %all-to-all-done = bf16[64,8,128]{2,1,0:T(8,128)(2,1)S(1)} async-done(((bf16[64,8,128]{2,1,0:T(8,128)(2,1)}), bf16[64,8,128]{2,1,0:T(8,128)(2,1)S(1)}, u32[]{:S(2)}, u32[]{:S(2)}) %all-to-all-start) | async-done | bytes 131104 | tf_op jit(solution)/shard_map/all_to_all | solution.py:298
  36.3 0.2 pick.1
  36.4 12.7 %all_to_all.25.got_ref = bf16[8,16,128]{2,1,0:T(8,128)(2,1)S(1)} all-to-all(bf16[8,16,128]{2,1,0:T(8,128)(2,1)S(1)} %pick.1), channel_id=1, replica_groups=mesh['takers'=64,'nodes'=8] {'nodes'}, dimensions={0} | all-to-all | bytes 65536 | tf_op jit(solution)/shard_map/all_to_all | solution.py:307
  49.1 0.0 copy-done
  49.1 0.1 dynamic-slice_bitcast_fusion.resp_ref
  49.2 7.3 %likelihood.1 = (f32[2048,128]{1,0:T(8,128)S(1)}, f32[8,128]{1,0:T(8,128)S(1)}) custom-call(s32[1]{0:T(128)} %bitcast.1.place_ref, bf16[8,16,128]{2,1,0:T(8,128)(2,1)S(1)} %all_to_all.25.got_ref, s32[12,128,128]{2,1,0:T(8,128)S(1)} %dynamic-slice_bitcast_fusion.resp_ref), custom_call_target="tpu_custom_call" | custom-call | tf_op jit(solution)/shard_map/likelihood/pallas_call | solution.py:309
  56.5 2.6 %collective-permute-start = (f32[8,128]{1,0:T(8,128)S(1)}, f32[8,128]{1,0:T(8,128)S(1)}, u32[]{:S(2)}, u32[]{:S(2)}) collective-permute-start(f32[8,128]{1,0:T(8,128)S(1)} %get-tuple-element.17.mine_ref), channel_id=1, source_target_pairs={{0,1},{1,0},{2,3},{3,2},{4,5},{5,4},{6,7},{7,6},{8,9},{9,8},{10,11... | collective-permute-start | bytes 12296 | tf_op jit(solution)/shard_map/ppermute | solution.py:324
  59.2 0.8 collective-permute-done.other_ref
  60.0 7.7 %statistics.1 = f32[8,16,128]{2,1,0:T(8,128)S(1)} custom-call(s32[1]{0:T(128)} %bitcast.1.place_ref, bf16[8,16,128]{2,1,0:T(8,128)(2,1)S(1)} %all_to_all.25.got_ref, s32[12,128,128]{2,1,0:T(8,128)S(1)} %dynamic-slice_bitcast_fusion.resp_ref, f32[2048,128]{1,0:T(8,128)S(1)} %get-tuple-element.16.w_ref, f32[8,128]{1,0:T(8,128)S(1)} %get-tuple-element.17.mine_ref, ...), custom_call_target="tpu_custom_call" | custom-call | tf_op jit(solution)/shard_map/statistics/pallas_call | solution.py:325
  67.7 7.6 %all_to_all.26.got_ref = f32[8,16,128]{2,1,0:T(8,128)S(1)} all-to-all(f32[8,16,128]{2,1,0:T(8,128)S(1)} %statistics.1), channel_id=1, replica_groups=mesh['takers'=64,'nodes'=8] {'nodes'}, dimensions={0} | all-to-all | bytes 131072 | tf_op jit(solution)/shard_map/all_to_all | solution.py:334
  75.3 0.6 spread.1
  75.9 19.1 %all_to_all.27.got_ref = bf16[64,8,128]{2,1,0:T(8,128)(2,1)S(1)} all-to-all(bf16[64,8,128]{2,1,0:T(8,128)(2,1)S(1)} %bitcast.10), channel_id=1, replica_groups=mesh['takers'=64,'nodes'=8] {'takers'}, dimensions={0} | all-to-all | bytes 262144 | tf_op jit(solution)/shard_map/all_to_all | solution.py:343
  95.0 0.1 gather.1
  95.1 10.5 %all_to_all.28.got_ref = f32[8,8,128]{2,1,0:T(8,128)S(1)} all-to-all(f32[8,8,128]{2,1,0:T(8,128)S(1)} %gather.1), channel_id=1, replica_groups=mesh['takers'=64,'nodes'=8] {'nodes'}, dimensions={0} | all-to-all | bytes 65536 | tf_op jit(solution)/shard_map/all_to_all | solution.py:359
  105.6 0.6 update.1
  (3 shorter events, 0.0 us)
Async XLA Ops:
  0.6 48.5 %copy-start = (s32[4,12,128,128]{3,2,1,0:T(8,128)S(1)}, s32[4,12,128,128]{3,2,1,0:T(8,128)}, u32[]{:S(2)}) copy-start(s32[4,12,128,128]{3,2,1,0:T(8,128)} %param.9) | copy-start | bytes 9437188
  0.6 104.9 %copy-start.1 = (bf16[3,1024]{1,0:T(4,128)(2,1)S(1)}, bf16[3,1024]{1,0:T(4,128)(2,1)}, u32[]{:S(2)}) copy-start(bf16[3,1024]{1,0:T(4,128)(2,1)} %slopes_ref.1) | copy-start | bytes 18436
  0.7 104.9 %copy-start.2 = (bf16[1024]{0:T(1024)(128)(2,1)S(1)}, bf16[1024]{0:T(1024)(128)(2,1)}, u32[]{:S(2)}) copy-start(bf16[1024]{0:T(1024)(128)(2,1)} %param.7) | copy-start | bytes 6148
  2.2 34.0 %all-to-all-start = ((bf16[64,8,128]{2,1,0:T(8,128)(2,1)}), bf16[64,8,128]{2,1,0:T(8,128)(2,1)S(1)}, u32[]{:S(2)}, u32[]{:S(2)}) async-start(bf16[64,8,128]{2,1,0:T(8,128)(2,1)} %offer.1), calls=%async_computation | async-start | bytes 262144 | tf_op jit(solution)/shard_map/all_to_all | solution.py:298
  21.4 0.7 copy-start.3
  22.0 0.7 copy-start.4
  56.5 3.4 %collective-permute-start = (f32[8,128]{1,0:T(8,128)S(1)}, f32[8,128]{1,0:T(8,128)S(1)}, u32[]{:S(2)}, u32[]{:S(2)}) collective-permute-start(f32[8,128]{1,0:T(8,128)S(1)} %get-tuple-element.17.mine_ref), channel_id=1, source_target_pairs={{0,1},{1,0},{2,3},{3,2},{4,5},{5,4},{6,7},{7,6},{8,9},{9,8},{10,11... | collective-permute-start | bytes 12296 | tf_op jit(solution)/shard_map/ppermute | solution.py:324

commit v4 on v3

--- a/solution.py
+++ b/solution.py
@@ -128,18 +128,23 @@
         for s in range(0, HERE, 4 * SLAB):
             w_ref[s : s + 4 * SLAB, :] += jnp.dot(tab_ref[s : s + 4 * SLAB, :], marks, preferred_element_type=F32)
 
+    def fill(pair, tab_ref, mark_ref):
+        for side in range(2):
+            k = 2 * pair + side
+            mark(k, mark_ref, 2 * TILE * side)
+            tables(k, tab_ref, 2 * TILE * side)
+
     def both(step, carry):
-        for half, (tab_ref, mark_ref) in enumerate(((tab_a, mark_a), (tab_b, mark_b))):
-            for side in range(2):
-                k = 4 * step + 2 * half + side
-                mark(k, mark_ref, 2 * TILE * side)
-                tables(k, tab_ref, 2 * TILE * side)
-            gather(*((tab_b, mark_b), (tab_a, mark_a))[half])
+        fill(2 * step + 1, tab_b, mark_b)
+        gather(tab_a, mark_a)
+        fill(2 * step + 2, tab_a, mark_a)
+        gather(tab_b, mark_b)
         return carry
 
-    tab_b[...] = jnp.zeros(tab_b.shape, BF16)
-    mark_b[...] = jnp.zeros(mark_b.shape, BF16)
-    lax.fori_loop(0, KT // 4, both, 0)
+    fill(0, tab_a, mark_a)
+    lax.fori_loop(0, KT // 4 - 1, both, 0)
+    fill(KT // 2 - 1, tab_b, mark_b)
+    gather(tab_a, mark_a)
     gather(tab_b, mark_b)
 
     top = jnp.full((SIDE, TILE), -jnp.inf, F32)
@@ -197,7 +202,7 @@
             counts = jnp.dot(post_ref[j0 * SLAB : (j0 + 1) * SLAB, :], marks, preferred_element_type=F32)
             theta0 = first + STEP * j0
             u = base
-            g_slab, f_slab = zero, zero_h
+            g_slab, f_slab, infos = zero, zero_h, []
             for j1 in range(SIDE):
                 hits = counts[j1 * SIDE : (j1 + 1) * SIDE, 0:TILE]
                 mass = counts[j1 * SIDE : (j1 + 1) * SIDE, TILE : 2 * TILE]
@@ -207,9 +212,12 @@
                 info = mass_sig * (share * miss)
                 g_slab = g_slab + (hits * share - mass_sig)
                 g_run = g_run + (g_slab[:HALF] + g_slab[HALF:])
-                info = info[:HALF] + info[HALF:]
-                f_slab = f_slab + info
-                f_1 = f_1 + float(AXIS[j1]) ** 2 * info
+                infos.append(info)
+                if j1 >= HALF:
+                    info = info + infos[SIDE - 1 - j1]
+                    info = info[:HALF] + info[HALF:]
+                    f_slab = f_slab + info
+                    f_1 = f_1 + float(AXIS[j1]) ** 2 * info
                 u = u * ratio1
             g_all, f_all = g_all + g_slab, f_all + f_slab
             g_0, f_0 = g_0 + theta0 * g_slab, f_0 + (theta0 * theta0) * f_slab
@@ -229,11 +237,9 @@
             tile(4 * step + side)
 
 
-def spread_kernel(turn_ref, got_ref, out_ref, marg_ref, mean_ref):
+def spread_kernel(turn_ref, got_ref, out_ref):
     both = []
     for b in range(4):
-        marg_ref[0:1, b * TILE : (b + 1) * TILE] = got_ref[2 * b, KT : KT + 1, :]
-        mean_ref[:, b * TILE : (b + 1) * TILE] = got_ref[2 * b, KT + 1 : KT + 4, :]
         both.append(got_ref[2 * b] + got_ref[2 * b + 1])
     both.extend([jnp.zeros((4 * SLOTS, TILE), F32)])
     both = jnp.concatenate(both, axis=0)
@@ -249,7 +255,10 @@
     out_ref[...] = jnp.broadcast_to(total[None], out_ref.shape)
 
 
-def update_kernel(slopes_ref, icpt_ref, got_ref, out_ref):
+def update_kernel(slopes_ref, icpt_ref, part_ref, got_ref, out_ref, marg_ref, mean_ref):
+    for b in range(4):
+        marg_ref[0:1, b * TILE : (b + 1) * TILE] = part_ref[2 * b, KT : KT + 1, :]
+        mean_ref[:, b * TILE : (b + 1) * TILE] = part_ref[2 * b, KT + 1 : KT + 4, :]
     slopes = slopes_ref[...].astype(F32)
     icpt = icpt_ref[...].astype(F32)
     for p in range(4):
@@ -332,11 +341,11 @@
         name="statistics",
     )(place, got, answers, weights, state, other)
     partial = lax.all_to_all(stats, "nodes", 0, 0)
-    spread, marginal, means = pl.pallas_call(
+    spread = pl.pallas_call(
         spread_kernel,
-        out_shape=(shape((blocks, TILE), BF16), shape((1, 4 * TILE)), shape((3, 4 * TILE))),
+        out_shape=shape((blocks, TILE), BF16),
         in_specs=[VMEM, VMEM],
-        out_specs=(VMEM, VMEM, VMEM),
+        out_specs=VMEM,
         compiler_params=params(4),
         name="spread",
     )(turn, partial)
@@ -349,14 +358,14 @@
         compiler_params=params(4),
         name="gather",
     )(owned)
-    new_params = pl.pallas_call(
+    new_params, marginal, means = pl.pallas_call(
         update_kernel,
-        out_shape=shape((4, own)),
-        in_specs=[VMEM, VMEM, VMEM],
-        out_specs=VMEM,
+        out_shape=(shape((4, own)), shape((1, 4 * TILE)), shape((3, 4 * TILE))),
+        in_specs=[VMEM, VMEM, VMEM, VMEM],
+        out_specs=(VMEM, VMEM, VMEM),
         compiler_params=params(4),
         name="update",
-    )(slopes, icpt, lax.all_to_all(summed, "nodes", 0, 0))
+    )(slopes, icpt, partial, lax.all_to_all(summed, "nodes", 0, 0))
     return new_params, marginal.reshape(-1), means
 
 

time: 107 us -> 105 us (0.981)
  Pallas kernels: 18.9 us -> 17.8 us
where the time goes in v4:
time: 105 us
  blocking collectives  49.9 us (48%)
  starting transfers between devices  21.8 us (21%)
  Pallas kernels  17.8 us (17%)
  waiting for transfers between devices  13.6 us (13%)
  local copies, waits for them, and re-layouts  1.4 us (1%)
    all_to_all x1, starting transfers between devices, local(): table = lax.all_to_all(offer, 'takers', 0, 0).reshape(blocks, TILE)  19.1 us
    all_to_all x1, blocking collectives, local(): owned = lax.all_to_all(spread.reshape(takers, rows, TILE), 'takers', 0, 0)  19.1 us
    all_to_all x1, waiting for transfers between devices, local(): table = lax.all_to_all(offer, 'takers', 0, 0).reshape(blocks, TILE)  12.8 us
    all_to_all x1, blocking collectives, local(): lax.all_to_all(picked, 'nodes', 0, 0)  12.7 us
    all_to_all x1, blocking collectives, local(): lax.all_to_all(summed, 'nodes', 0, 0)  10.5 us
    all_to_all x1, blocking collectives, local(): partial = lax.all_to_all(stats, 'nodes', 0, 0)  7.55 us
    pallas_call x1, Pallas kernels, local(): pl.pallas_call(statistics_kernel, out_shape=shape((8, SLOTS, TILE)), in_s...  7.55 us
    pallas_call x1, Pallas kernels, local(): pl.pallas_call(likelihood_kernel, out_shape=(shape((HERE, TILE)), shape((...  6.86 us
  transfers between devices with their start and end apart: 2, of which 2 were waited for; matrix products, arithmetic and copies ran while one was open for 0% of the time, Pallas kernels for 1%

profile of v4, /device:TPU:1, one launch (start us, length us, event | category | flops | bytes accessed | tf_op | source)
XLA Modules:
  0.0 105.1 jit_solution(9575067924557885749)
XLA Ops:
  0.6 0.0 copy-start
  0.6 0.0 copy-start.1
  0.7 0.0 copy-start.2
  0.7 1.6 %offer.1 = bf16[64,8,128]{2,1,0:T(8,128)(2,1)} custom-call(s32[1]{0:T(128)} %bitcast.1.place_ref, bf16[3,1024]{1,0:T(4,128)(2,1)} %slopes_ref.1, bf16[8,128]{1,0:T(8,128)(2,1)} %bitcast.11, bf16[8,128]{1,0:T(8,128)(2,1)} %bitcast.13), custom_call_target="tpu_custom_call" | custom-call | tf_op jit(solution)/shard_map/offer/pallas_call | solution.py:284
  2.2 19.1 %all-to-all-start = ((bf16[64,8,128]{2,1,0:T(8,128)(2,1)}), bf16[64,8,128]{2,1,0:T(8,128)(2,1)S(1)}, u32[]{:S(2)}, u32[]{:S(2)}) async-start(bf16[64,8,128]{2,1,0:T(8,128)(2,1)} %offer.1), calls=%async_computation | async-start | bytes 262144 | tf_op jit(solution)/shard_map/all_to_all | solution.py:307
  21.4 0.0 copy-start.3
  21.4 0.7 copy-done.3
  22.0 0.7 copy-done.4
  22.7 0.8 plan.1
  23.5 12.8 %all-to-all-done = bf16[64,8,128]{2,1,0:T(8,128)(2,1)S(1)} async-done(((bf16[64,8,128]{2,1,0:T(8,128)(2,1)}), bf16[64,8,128]{2,1,0:T(8,128)(2,1)S(1)}, u32[]{:S(2)}, u32[]{:S(2)}) %all-to-all-start) | async-done | bytes 131104 | tf_op jit(solution)/shard_map/all_to_all | solution.py:307
  36.3 0.2 pick.1
  36.4 12.7 %all_to_all.25.got_ref = bf16[8,16,128]{2,1,0:T(8,128)(2,1)S(1)} all-to-all(bf16[8,16,128]{2,1,0:T(8,128)(2,1)S(1)} %pick.1), channel_id=1, replica_groups=mesh['takers'=64,'nodes'=8] {'nodes'}, dimensions={0} | all-to-all | bytes 65536 | tf_op jit(solution)/shard_map/all_to_all | solution.py:316
  49.1 0.0 copy-done
  49.1 0.1 dynamic-slice_bitcast_fusion.resp_ref
  49.2 6.9 %likelihood.1 = (f32[2048,128]{1,0:T(8,128)S(1)}, f32[8,128]{1,0:T(8,128)S(1)}) custom-call(s32[1]{0:T(128)} %bitcast.1.place_ref, bf16[8,16,128]{2,1,0:T(8,128)(2,1)S(1)} %all_to_all.25.got_ref, s32[12,128,128]{2,1,0:T(8,128)S(1)} %dynamic-slice_bitcast_fusion.resp_ref), custom_call_target="tpu_custom_call" | custom-call | tf_op jit(solution)/shard_map/likelihood/pallas_call | solution.py:318
  56.1 2.6 %collective-permute-start = (f32[8,128]{1,0:T(8,128)S(1)}, f32[8,128]{1,0:T(8,128)S(1)}, u32[]{:S(2)}, u32[]{:S(2)}) collective-permute-start(f32[8,128]{1,0:T(8,128)S(1)} %get-tuple-element.16.mine_ref), channel_id=1, source_target_pairs={{0,1},{1,0},{2,3},{3,2},{4,5},{5,4},{6,7},{7,6},{8,9},{9,8},{10,11... | collective-permute-start | bytes 12296 | tf_op jit(solution)/shard_map/ppermute | solution.py:333
  58.7 0.8 collective-permute-done.other_ref
  59.5 7.5 %statistics.1 = f32[8,16,128]{2,1,0:T(8,128)S(1)} custom-call(s32[1]{0:T(128)} %bitcast.1.place_ref, bf16[8,16,128]{2,1,0:T(8,128)(2,1)S(1)} %all_to_all.25.got_ref, s32[12,128,128]{2,1,0:T(8,128)S(1)} %dynamic-slice_bitcast_fusion.resp_ref, f32[2048,128]{1,0:T(8,128)S(1)} %get-tuple-element.15.w_ref, f32[8,128]{1,0:T(8,128)S(1)} %get-tuple-element.16.mine_ref, ...), custom_call_target="tpu_custom_call" | custom-call | tf_op jit(solution)/shard_map/statistics/pallas_call | solution.py:334
  67.1 7.5 %all_to_all.26.got_ref.part_ref = f32[8,16,128]{2,1,0:T(8,128)S(1)} all-to-all(f32[8,16,128]{2,1,0:T(8,128)S(1)} %statistics.1), channel_id=1, replica_groups=mesh['takers'=64,'nodes'=8] {'nodes'}, dimensions={0} | all-to-all | bytes 131072 | tf_op jit(solution)/shard_map/all_to_all | solution.py:343
  74.6 0.2 spread.1
  74.8 19.1 %all_to_all.27.got_ref = bf16[64,8,128]{2,1,0:T(8,128)(2,1)S(1)} all-to-all(bf16[64,8,128]{2,1,0:T(8,128)(2,1)S(1)} %bitcast.10), channel_id=1, replica_groups=mesh['takers'=64,'nodes'=8] {'takers'}, dimensions={0} | all-to-all | bytes 262144 | tf_op jit(solution)/shard_map/all_to_all | solution.py:352
  93.9 0.1 gather.1
  94.0 10.5 %all_to_all.28.got_ref = f32[8,8,128]{2,1,0:T(8,128)S(1)} all-to-all(f32[8,8,128]{2,1,0:T(8,128)S(1)} %gather.1), channel_id=1, replica_groups=mesh['takers'=64,'nodes'=8] {'nodes'}, dimensions={0} | all-to-all | bytes 65536 | tf_op jit(solution)/shard_map/all_to_all | solution.py:368
  104.5 0.6 update.1
  (3 shorter events, 0.0 us)
Async XLA Ops:
  0.6 48.5 %copy-start = (s32[4,12,128,128]{3,2,1,0:T(8,128)S(1)}, s32[4,12,128,128]{3,2,1,0:T(8,128)}, u32[]{:S(2)}) copy-start(s32[4,12,128,128]{3,2,1,0:T(8,128)} %param.9) | copy-start | bytes 9437188
  0.6 103.8 %copy-start.1 = (bf16[3,1024]{1,0:T(4,128)(2,1)S(1)}, bf16[3,1024]{1,0:T(4,128)(2,1)}, u32[]{:S(2)}) copy-start(bf16[3,1024]{1,0:T(4,128)(2,1)} %slopes_ref.1) | copy-start | bytes 18436
  0.7 103.8 %copy-start.2 = (bf16[1024]{0:T(1024)(128)(2,1)S(1)}, bf16[1024]{0:T(1024)(128)(2,1)}, u32[]{:S(2)}) copy-start(bf16[1024]{0:T(1024)(128)(2,1)} %param.7) | copy-start | bytes 6148
  2.2 34.0 %all-to-all-start = ((bf16[64,8,128]{2,1,0:T(8,128)(2,1)}), bf16[64,8,128]{2,1,0:T(8,128)(2,1)S(1)}, u32[]{:S(2)}, u32[]{:S(2)}) async-start(bf16[64,8,128]{2,1,0:T(8,128)(2,1)} %offer.1), calls=%async_computation | async-start | bytes 262144 | tf_op jit(solution)/shard_map/all_to_all | solution.py:307
  21.4 0.7 copy-start.3
  22.0 0.7 copy-start.4
  56.1 3.5 %collective-permute-start = (f32[8,128]{1,0:T(8,128)S(1)}, f32[8,128]{1,0:T(8,128)S(1)}, u32[]{:S(2)}, u32[]{:S(2)}) collective-permute-start(f32[8,128]{1,0:T(8,128)S(1)} %get-tuple-element.16.mine_ref), channel_id=1, source_target_pairs={{0,1},{1,0},{2,3},{3,2},{4,5},{5,4},{6,7},{7,6},{8,9},{9,8},{10,11... | collective-permute-start | bytes 12296 | tf_op jit(solution)/shard_map/ppermute | solution.py:333

commit v5 on v4

--- a/solution.py
+++ b/solution.py
@@ -170,7 +170,15 @@
     st_ref[5:8, :] = jnp.zeros((3, TILE), F32)
 
 
-def statistics_kernel(place_ref, got_ref, resp_ref, w_ref, mine_ref, other_ref, out_ref, par_ref, post_ref):
+def marks_kernel(got_ref, resp_ref, out_ref):
+    live = got_ref[5].astype(F32)
+    for k in range(KT):
+        codes, used = resp_ref[k], live[k : k + 1]
+        out_ref[k, :, 0:TILE] = jnp.where(codes == 2, used, 0.0).astype(BF16)
+        out_ref[k, :, TILE : 2 * TILE] = jnp.where(codes > 0, used, 0.0).astype(BF16)
+
+
+def statistics_kernel(place_ref, got_ref, marks_ref, w_ref, mine_ref, other_ref, out_ref, par_ref, post_ref):
     first = first_theta0(place_ref)
     par_ref[...] = got_ref[...].astype(F32)
     mine, other = mine_ref[...], other_ref[...]
@@ -188,27 +196,26 @@
     zero_h = jnp.zeros((HALF, TILE), F32)
 
     def tile(k):
-        a0, a1, a2, d, c, live = (par_ref[j, pl.ds(k, 1), :] for j in range(6))
-        codes = resp_ref[k]
-        hit, any_answer = jnp.where(codes == 2, live, 0.0), jnp.where(codes > 0, live, 0.0)
-        marks = jnp.concatenate([hit.astype(BF16), any_answer.astype(BF16)], axis=1)
-        base = jnp.exp(a2 * theta2 + (a0 * first + a1 * float(AXIS[0]) + d))
-        ratio0 = jnp.broadcast_to(jnp.exp(a0 * STEP), (SIDE, TILE))
-        ratio1 = jnp.broadcast_to(jnp.exp(a1 * STEP), (SIDE, TILE))
+        a0, a1, a2, d, c = (par_ref[j, pl.ds(k, 1), :] for j in range(5))
+        marks = marks_ref[k]
+        base = jnp.exp(-(a2 * theta2 + (a0 * first + a1 * float(AXIS[0]) + d)))
+        ratio0 = jnp.broadcast_to(jnp.exp(a0 * -STEP), (SIDE, TILE))
+        ratio1 = jnp.broadcast_to(jnp.exp(a1 * -STEP), (SIDE, TILE))
         c_b = jnp.broadcast_to(c, (SIDE, TILE))
         g_all, g_0, g_run = zero, zero, zero_h
         f_all, f_0, f_1 = zero_h, zero_h, zero_h
         for j0 in range(HALF):
             counts = jnp.dot(post_ref[j0 * SLAB : (j0 + 1) * SLAB, :], marks, preferred_element_type=F32)
             theta0 = first + STEP * j0
-            u = base
+            e, ce = base, base * c_b
             g_slab, f_slab, infos = zero, zero_h, []
             for j1 in range(SIDE):
                 hits = counts[j1 * SIDE : (j1 + 1) * SIDE, 0:TILE]
                 mass = counts[j1 * SIDE : (j1 + 1) * SIDE, TILE : 2 * TILE]
-                miss = 1.0 / (1.0 + u)
-                share = u * (1.0 / (c_b + u))
-                mass_sig = mass * (u * miss)
+                sig = 1.0 / (1.0 + e)
+                share = 1.0 / (1.0 + ce)
+                miss = e * sig
+                mass_sig = mass * sig
                 info = mass_sig * (share * miss)
                 g_slab = g_slab + (hits * share - mass_sig)
                 g_run = g_run + (g_slab[:HALF] + g_slab[HALF:])
@@ -218,7 +225,7 @@
                     info = info[:HALF] + info[HALF:]
                     f_slab = f_slab + info
                     f_1 = f_1 + float(AXIS[j1]) ** 2 * info
-                u = u * ratio1
+                e, ce = e * ratio1, ce * ratio1
             g_all, f_all = g_all + g_slab, f_all + f_slab
             g_0, f_0 = g_0 + theta0 * g_slab, f_0 + (theta0 * theta0) * f_slab
             base = base * ratio0
@@ -231,10 +238,10 @@
             summed = jnp.sum(part, axis=0, keepdims=True)
             out_ref[j, pl.ds(k, 1), :] = summed if j < 4 else summed * rest
 
-    @pl.loop(0, KT // 4)
+    @pl.loop(0, KT // 6)
     def _(step):
-        for side in range(4):
-            tile(4 * step + side)
+        for side in range(6):
+            tile(6 * step + side)
 
 
 def spread_kernel(turn_ref, got_ref, out_ref):
@@ -330,7 +337,16 @@
         compiler_params=params(14),
         name="likelihood",
     )(place, got, answers)
+    state, answers = lax.optimization_barrier((state, answers))
     other = lax.ppermute(state, "nodes", [(i, i ^ 1) for i in range(8)])
+    marks = pl.pallas_call(
+        marks_kernel,
+        out_shape=shape((KT, TILE, 2 * TILE), BF16),
+        in_specs=[VMEM, VMEM],
+        out_specs=VMEM,
+        compiler_params=params(6),
+        name="marks",
+    )(got, answers)
     stats = pl.pallas_call(
         statistics_kernel,
         out_shape=shape((8, SLOTS, TILE)),
@@ -339,7 +355,7 @@
         scratch_shapes=[pltpu.VMEM((8, SLOTS, TILE), F32), pltpu.VMEM((HERE, TILE), BF16)],
         compiler_params=params(14),
         name="statistics",
-    )(place, got, answers, weights, state, other)
+    )(place, got, marks, weights, state, other)
     partial = lax.all_to_all(stats, "nodes", 0, 0)
     spread = pl.pallas_call(
         spread_kernel,

time: 105 us -> 105 us (level)
  no operation moved by 1% of the time
where the time goes in v5:
time: 105 us
  blocking collectives  49.9 us (48%)
  starting transfers between devices  21.8 us (21%)
  Pallas kernels  17.7 us (17%)
  waiting for transfers between devices  13.4 us (13%)
  local copies, waits for them, and re-layouts  1.4 us (1%)
    all_to_all x1, starting transfers between devices, local(): table = lax.all_to_all(offer, 'takers', 0, 0).reshape(blocks, TILE)  19.1 us
    all_to_all x1, blocking collectives, local(): owned = lax.all_to_all(spread.reshape(takers, rows, TILE), 'takers', 0, 0)  19.1 us
    all_to_all x1, waiting for transfers between devices, local(): table = lax.all_to_all(offer, 'takers', 0, 0).reshape(blocks, TILE)  12.8 us
    all_to_all x1, blocking collectives, local(): lax.all_to_all(picked, 'nodes', 0, 0)  12.7 us
    all_to_all x1, blocking collectives, local(): lax.all_to_all(summed, 'nodes', 0, 0)  10.5 us
    all_to_all x1, blocking collectives, local(): partial = lax.all_to_all(stats, 'nodes', 0, 0)  7.56 us
    pallas_call x1, Pallas kernels, local(): pl.pallas_call(statistics_kernel, out_shape=shape((8, SLOTS, TILE)), in_s...  7.23 us
    pallas_call x1, Pallas kernels, local(): pl.pallas_call(likelihood_kernel, out_shape=(shape((HERE, TILE)), shape((...  6.85 us
  transfers between devices with their start and end apart: 2, of which 2 were waited for; matrix products, arithmetic and copies ran while one was open for 0% of the time, Pallas kernels for 1%

profile of v5, /device:TPU:1, one launch (start us, length us, event | category | flops | bytes accessed | tf_op | source)
XLA Modules:
  0.0 104.8 jit_solution(1551106214123062861)
XLA Ops:
  0.6 0.0 copy-start
  0.6 1.6 %offer.1 = bf16[64,8,128]{2,1,0:T(8,128)(2,1)} custom-call(s32[1]{0:T(128)} %bitcast.1.place_ref, bf16[3,1024]{1,0:T(4,128)(2,1)} %slopes_ref.1, bf16[8,128]{1,0:T(8,128)(2,1)} %bitcast.11, bf16[8,128]{1,0:T(8,128)(2,1)} %bitcast.13), custom_call_target="tpu_custom_call" | custom-call | tf_op jit(solution)/shard_map/offer/pallas_call | solution.py:291
  2.2 19.1 %all-to-all-start = ((bf16[64,8,128]{2,1,0:T(8,128)(2,1)}), bf16[64,8,128]{2,1,0:T(8,128)(2,1)S(1)}, u32[]{:S(2)}, u32[]{:S(2)}) async-start(bf16[64,8,128]{2,1,0:T(8,128)(2,1)} %offer.1), calls=%async_computation | async-start | bytes 262144 | tf_op jit(solution)/shard_map/all_to_all | solution.py:314
  21.3 0.0 copy-start.3
  21.4 0.7 copy-done.3
  22.0 0.7 copy-done.4
  22.7 0.8 plan.1
  23.5 12.8 %all-to-all-done = bf16[64,8,128]{2,1,0:T(8,128)(2,1)S(1)} async-done(((bf16[64,8,128]{2,1,0:T(8,128)(2,1)}), bf16[64,8,128]{2,1,0:T(8,128)(2,1)S(1)}, u32[]{:S(2)}, u32[]{:S(2)}) %all-to-all-start) | async-done | bytes 131104 | tf_op jit(solution)/shard_map/all_to_all | solution.py:314
  36.2 0.2 pick.1
  36.4 12.7 %all_to_all.25.got_ref = bf16[8,16,128]{2,1,0:T(8,128)(2,1)S(1)} all-to-all(bf16[8,16,128]{2,1,0:T(8,128)(2,1)S(1)} %pick.1), channel_id=1, replica_groups=mesh['takers'=64,'nodes'=8] {'nodes'}, dimensions={0} | all-to-all | bytes 65536 | tf_op jit(solution)/shard_map/all_to_all | solution.py:323
  49.1 0.0 copy-done
  49.1 0.1 dynamic-slice_bitcast_fusion.resp_ref
  49.2 6.9 %likelihood.1 = (f32[2048,128]{1,0:T(8,128)S(1)}, f32[8,128]{1,0:T(8,128)S(1)}) custom-call(s32[1]{0:T(128)} %bitcast.1.place_ref, bf16[8,16,128]{2,1,0:T(8,128)(2,1)S(1)} %all_to_all.25.got_ref, s32[12,128,128]{2,1,0:T(8,128)S(1)} %dynamic-slice_bitcast_fusion.resp_ref), custom_call_target="tpu_custom_call" | custom-call | tf_op jit(solution)/shard_map/likelihood/pallas_call | solution.py:325
  56.0 2.6 %collective-permute-start = (f32[8,128]{1,0:T(8,128)S(1)}, f32[8,128]{1,0:T(8,128)S(1)}, u32[]{:S(2)}, u32[]{:S(2)}) collective-permute-start(f32[8,128]{1,0:T(8,128)S(1)} %get-tuple-element.20.mine_ref), channel_id=1, source_target_pairs={{0,1},{1,0},{2,3},{3,2},{4,5},{5,4},{6,7},{7,6},{8,9},{9,8},{10,11... | collective-permute-start | bytes 12296 | tf_op jit(solution)/shard_map/ppermute | solution.py:341
  58.7 0.2 marks.1.marks_ref
  58.9 0.6 collective-permute-done.other_ref
  59.5 7.2 %statistics.1 = f32[8,16,128]{2,1,0:T(8,128)S(1)} custom-call(s32[1]{0:T(128)} %bitcast.1.place_ref, bf16[8,16,128]{2,1,0:T(8,128)(2,1)S(1)} %all_to_all.25.got_ref, bf16[12,128,256]{2,1,0:T(8,128)(2,1)S(1)} %marks.1.marks_ref, f32[2048,128]{1,0:T(8,128)S(1)} %get-tuple-element.19.w_ref, f32[8,128]{1,0:T(8,128)S(1)} %get-tuple-element.20.mine_ref, ...), custom_call_target="tpu_custom_call" | custom-call | tf_op jit(solution)/shard_map/statistics/pallas_call | solution.py:350
  66.7 7.6 %all_to_all.26.got_ref.part_ref = f32[8,16,128]{2,1,0:T(8,128)S(1)} all-to-all(f32[8,16,128]{2,1,0:T(8,128)S(1)} %statistics.1), channel_id=1, replica_groups=mesh['takers'=64,'nodes'=8] {'nodes'}, dimensions={0} | all-to-all | bytes 131072 | tf_op jit(solution)/shard_map/all_to_all | solution.py:359
  74.3 0.2 spread.1
  74.5 19.1 %all_to_all.27.got_ref = bf16[64,8,128]{2,1,0:T(8,128)(2,1)S(1)} all-to-all(bf16[64,8,128]{2,1,0:T(8,128)(2,1)S(1)} %bitcast.10), channel_id=1, replica_groups=mesh['takers'=64,'nodes'=8] {'takers'}, dimensions={0} | all-to-all | bytes 262144 | tf_op jit(solution)/shard_map/all_to_all | solution.py:368
  93.6 0.1 gather.1
  93.7 10.5 %all_to_all.28.got_ref = f32[8,8,128]{2,1,0:T(8,128)S(1)} all-to-all(f32[8,8,128]{2,1,0:T(8,128)S(1)} %gather.1), channel_id=1, replica_groups=mesh['takers'=64,'nodes'=8] {'nodes'}, dimensions={0} | all-to-all | bytes 65536 | tf_op jit(solution)/shard_map/all_to_all | solution.py:384
  104.2 0.0 copy-done.2
  104.2 0.6 update.1
  (4 shorter events, 0.0 us)
Async XLA Ops:
  0.6 48.5 %copy-start = (s32[4,12,128,128]{3,2,1,0:T(8,128)S(1)}, s32[4,12,128,128]{3,2,1,0:T(8,128)}, u32[]{:S(2)}) copy-start(s32[4,12,128,128]{3,2,1,0:T(8,128)} %param.9) | copy-start | bytes 9437188
  2.2 34.0 %all-to-all-start = ((bf16[64,8,128]{2,1,0:T(8,128)(2,1)}), bf16[64,8,128]{2,1,0:T(8,128)(2,1)S(1)}, u32[]{:S(2)}, u32[]{:S(2)}) async-start(bf16[64,8,128]{2,1,0:T(8,128)(2,1)} %offer.1), calls=%async_computation | async-start | bytes 262144 | tf_op jit(solution)/shard_map/all_to_all | solution.py:314
  21.3 0.7 copy-start.3
  22.0 0.7 copy-start.4
  49.1 55.0 %copy-start.1 = (bf16[3,1024]{1,0:T(4,128)(2,1)S(1)}, bf16[3,1024]{1,0:T(4,128)(2,1)}, u32[]{:S(2)}) copy-start(bf16[3,1024]{1,0:T(4,128)(2,1)} %slopes_ref.1) | copy-start | bytes 18436
  49.1 55.0 %copy-start.2 = (bf16[1024]{0:T(1024)(128)(2,1)S(1)}, bf16[1024]{0:T(1024)(128)(2,1)}, u32[]{:S(2)}) copy-start(bf16[1024]{0:T(1024)(128)(2,1)} %param.7) | copy-start | bytes 6148
  56.0 3.5 %collective-permute-start = (f32[8,128]{1,0:T(8,128)S(1)}, f32[8,128]{1,0:T(8,128)S(1)}, u32[]{:S(2)}, u32[]{:S(2)}) collective-permute-start(f32[8,128]{1,0:T(8,128)S(1)} %get-tuple-element.20.mine_ref), channel_id=1, source_target_pairs={{0,1},{1,0},{2,3},{3,2},{4,5},{5,4},{6,7},{7,6},{8,9},{9,8},{10,11... | collective-permute-start | bytes 12296 | tf_op jit(solution)/shard_map/ppermute | solution.py:341
